TPU v7x, 32 devices: a whole 2x2x4 slice. The times are simulated.
32 devices in a mesh: group: 4 (over y, x), dp: 2 (over core), tensor: 4 (over z).
Axes of the slice: x: 2, y: 2, z: 4, core: 2. Of those that a mesh axis runs over, the one named last changes fastest.
Arguments:
- tokens: bfloat16 [8192, 2048], P(('group', 'dp')), may hold values from -6 to 6
- norm_gain: bfloat16 [2048], replicated, may hold values from 0.099609375 to 1.8984375
- w_query: bfloat16 [2048, 2048], P(None, 'tensor'), may hold values from -0.25 to 0.25
- w_keyval: bfloat16 [2048, 512], P(None, 'tensor'), may hold values from -0.125 to 0.125
- w_out: bfloat16 [2048, 2048], P('tensor'), may hold values from -0.8984375 to 0.8984375
- kv_cache: bfloat16 [4, 32, 16, 128, 512], P(None, ('group', 'dp'), None, None, 'tensor'), may hold values from -400 to 400
- lengths: int32 [32, 2], P(('group', 'dp')), may hold values from 0 to 2048, as said below
- dest_slot: int32 [32, 16], replicated, may hold values from 0 to 511, as said below
Outputs:
- mixed: bfloat16 [8192, 2048], P(('group', 'dp', 'tensor'))
- decode_cache: bfloat16 [4, 512, 128, 512], P(None, ('group', 'dp'), None, 'tensor')
Inputs may be any that keep to these rules, and one draw needn't show every extreme that they name: lengths[p, 0] lies in 0 to 2048 and lengths[p, 1] in 1 to 256; 2048 and 256 are each taken by some prompt; the prompts r * 4 to r * 4 + 3 of each index r of group and dp together hold exactly 32 live blocks. dest_slot is a permutation of the 512 slots; the slots of the index r of group and dp together are r * 4 * 16 onward; the blocks of prompts r * 4 to r * 4 + 3 send exactly 8 blocks to each index, of which exactly 4 is live.
All inputs are finite; a program needn't handle non-finite values.
Results may differ from a plain program's by a relative error of at most 0.009.
Values may be sent and summed in bfloat16 or wider, within the bound.
A program may use at most 128 MiB of HBM per device.

v0:
```python
import jax
import jax.numpy as jnp
from jax import lax
from jax.sharding import PartitionSpec as P

HD = 64


def per_device(tokens, norm_gain, w_query, w_keyval, w_out, kv_cache, lengths, dest_slot):
    tok_rows = tokens.shape[0]
    prompts = lengths.shape[0]
    fresh_rows = tok_rows // prompts
    heads_local = w_query.shape[1] // HD
    kv_local = w_keyval.shape[1] // (2 * HD)
    group_size = heads_local // kv_local
    layers = kv_cache.shape[0]
    blocks_win = kv_cache.shape[2]
    block_len = kv_cache.shape[3]
    lane_width = kv_cache.shape[4]
    window = blocks_win * block_len
    tokens_f = tokens.astype(jnp.float32)
    normed = (
        tokens_f
        * lax.rsqrt(jnp.mean(tokens_f * tokens_f, axis=-1, keepdims=True) + 1e-05)
        * norm_gain.astype(jnp.float32)
    ).astype(jnp.bfloat16)
    query = jnp.dot(normed, w_query, preferred_element_type=jnp.float32).astype(jnp.bfloat16)
    query = query.reshape(prompts, fresh_rows, kv_local, group_size, HD)
    keyval = jnp.dot(normed, w_keyval, preferred_element_type=jnp.float32).astype(jnp.bfloat16)
    keyval = keyval.reshape(prompts, fresh_rows, kv_local, 2, HD)
    cache = kv_cache[0].reshape(prompts, window, kv_local, 2, HD)
    scale = 1.0 / HD**0.5
    query_pos = jnp.arange(fresh_rows)[:, None]
    key_pos = jnp.arange(window + fresh_rows)[None, :]

    def attend(items):
        query_p, cache_p, fresh_p, history, fresh_len = items
        pairs = jnp.concatenate([cache_p, fresh_p], axis=0)
        scores = (
            jnp.einsum(
                "ckgd,tkd->kgct", query_p, pairs[:, :, 0], preferred_element_type=jnp.float32
            )
            * scale
        )
        visible = jnp.where(
            key_pos < window,
            (key_pos >= window - history) & (key_pos >= query_pos + 1),
            key_pos - window <= query_pos,
        )
        scores = jnp.where(visible, scores, -1e30)
        scores = scores - jnp.max(scores, axis=-1, keepdims=True)
        expo = jnp.exp(scores)
        weights = (expo / jnp.sum(expo, axis=-1, keepdims=True)).astype(jnp.bfloat16)
        mixed_p = jnp.einsum(
            "kgct,tkd->ckgd", weights, pairs[:, :, 1], preferred_element_type=jnp.float32
        )
        mixed_p = mixed_p.astype(jnp.bfloat16).reshape(fresh_rows, heads_local * HD)
        return jnp.where(
            (jnp.arange(fresh_rows) < fresh_len)[:, None], mixed_p, jnp.zeros_like(mixed_p)
        )

    attn = lax.map(attend, (query, cache, keyval, lengths[:, 0], lengths[:, 1]))
    attn = attn.reshape(tok_rows, heads_local * HD)
    mixed = lax.psum_scatter(
        jnp.dot(attn, w_out, preferred_element_type=jnp.float32),
        "tensor",
        scatter_dimension=0,
        tiled=True,
    ).astype(jnp.bfloat16)
    per_dev = prompts * blocks_win
    devices = lax.axis_size(("group", "dp"))
    per_peer = per_dev // devices
    my_index = lax.axis_index(("group", "dp"))
    dest_all = dest_slot.reshape(devices, per_dev)
    recv_all = dest_all // per_dev
    same_dest = recv_all[:, :, None] == recv_all[:, None, :]
    earlier = jnp.arange(per_dev)[None, :] < jnp.arange(per_dev)[:, None]
    own_recv = lax.dynamic_index_in_dim(recv_all, my_index, 0, keepdims=False)
    senders = jnp.arange(devices, dtype=jnp.int32)[:, None]
    capacity = per_peer // 2
    lengths_every = lax.all_gather(lengths, ("group", "dp"), axis=0, tiled=True)
    live_all = (
        (jnp.arange(blocks_win)[None, :] + 1) * block_len > window - lengths_every[:, 0:1]
    ).reshape(devices, per_dev)
    live_rank = jnp.sum(same_dest & earlier[None, :, :] & live_all[:, None, :], axis=2)
    own_live = lax.dynamic_index_in_dim(live_all, my_index, 0, keepdims=False)
    own_live_rank = lax.dynamic_index_in_dim(live_rank, my_index, 0, keepdims=False)
    send_pos = jnp.where(own_live, own_recv * capacity + own_live_rank, devices * capacity)
    send_idx = (
        jnp.zeros((devices * capacity,), jnp.int32)
        .at[send_pos]
        .set(jnp.arange(per_dev, dtype=jnp.int32), mode="drop")
    )
    raw_blocks = kv_cache.reshape(layers, per_dev, block_len, lane_width)
    outgoing = jnp.take(raw_blocks, send_idx, axis=1)
    incoming = lax.all_to_all(outgoing, ("group", "dp"), split_axis=1, concat_axis=1, tiled=True)
    where_from = senders * capacity + live_rank
    valid = (recv_all == my_index) & live_all
    slot_local = jnp.where(valid, dest_all - my_index * per_dev, per_dev)
    source_idx = (
        jnp.full((per_dev,), devices * capacity, jnp.int32)
        .at[slot_local.reshape(-1)]
        .set(where_from.reshape(-1), mode="drop")
    )
    decode_cache = jnp.take(incoming, source_idx, axis=1, mode="fill", fill_value=0)
    return (mixed, decode_cache)


def solution(mesh):
    in_specs = (
        P(("group", "dp"), None),
        P(),
        P(None, "tensor"),
        P(None, "tensor"),
        P("tensor", None),
        P(None, ("group", "dp"), None, None, "tensor"),
        P(("group", "dp"), None),
        P(),
    )
    out_specs = (P(("group", "dp", "tensor"), None), P(None, ("group", "dp"), None, "tensor"))
    return jax.shard_map(
        per_device, mesh=mesh, in_specs=in_specs, out_specs=out_specs, check_vma=False
    )
```

profile of v0, /device:TPU:6, one launch (start us, length us, event | category | flops | bytes accessed | tf_op | source)
XLA Modules:
  0.0 343.0 jit_solution(16174500329635103676)
XLA Ops:
  7.2 1.4 slice_bitcast_fusion
  8.6 3.2 slice.25
  11.8 4.5 %copy.51 = bf16[1,4,16,128,128]{3,2,4,1,0:T(8,128)(2,1)} copy(bf16[1,4,16,128,128]{4,3,2,1,0:T(8,128)(2,1)} %slice.25) | data formatting | bytes 4194304 | tf_op jit(solution)/shard_map/slice | solution.py:31
  16.3 4.2 %reshape_squeeze.3 = bf16[4,2048,1,2,64]{1,4,3,2,0:T(8,128)(2,1)} reshape(bf16[1,4,16,128,128]{3,2,4,1,0:T(8,128)(2,1)} %copy.51) | data formatting | bytes 4194304 | tf_op jit(solution)/shard_map/reshape;squeeze | solution.py:31
  20.4 3.1 fusion.27
  23.5 3.6 %fusion.33 = bf16[1024,128]{1,0:T(8,128)(2,1)S(1)} fusion(bf16[2048,128]{1,0:T(8,128)(2,1)} %param.13, bf16[1024,2048]{1,0:T(8,128)(2,1)} %param.10, f32[2048]{0:T(1024)S(1)} %convert_element_type.40, f32[1024]{0:T(1024)S(1)} %add_rsqrt_fusion), kind=kOutput, calls=%fused_computation.51 | convolution fusion | flops 545390592 | bytes 4993024 | tf_op jit(solution)/shard_map/dot_general | solution.py:29
  27.7 5.2 %convolution_convert_fusion = bf16[1024,512]{1,0:T(8,128)(2,1)S(1)} fusion(bf16[2048,512]{1,0:T(8,128)(2,1)} %param.12, bf16[1024,2048]{1,0:T(8,128)(2,1)} %param.10, f32[2048]{0:T(1024)S(1)} %convert_element_type.40, f32[1024]{0:T(1024)S(1)} %add_rsqrt_fusion), kind=kOutput, calls=%fused_computation.49 | convolution fusion | flops 2156396544 | bytes 7352320 | tf_op jit(solution)/shard_map/dot_general | solution.py:27
  33.0 2.1 reshape.481
  35.1 3.0 copy.55
  38.1 142.6 %while.14 = (s32[]{:T(128)}, bf16[4,256,512]{2,1,0:T(8,128)(2,1)}, s32[4]{0:T(128)}, bf16[4,2048,1,2,64]{1,4,3,2,0:T(8,128)(2,1)}, bf16[4,256,1,2,64]{1,4,3,2,0:...) while((s32[]{:T(128)}, bf16[4,256,512]{2,1,0:T(8,128)(2,1)}, ...), condition=%wide.region_4.5_spmd.clone.clone, body=%wide.region_1.4_spmd.clone.clone.sunk | while | flops 1268387072 | bytes 63510268 | solution.py:62
  38.1 1.3 dynamic_slice.91
  40.1 2.0 fusion.58
  42.2 1.1 dynamic-slice_bitcast_fusion.5
  43.3 9.0 %fusion.59 = (f32[8,256]{1,0:T(8,128)S(1)}, f32[2304,256,8]{1,0,2:T(8,128)}) fusion(pred[256,2304]{0,1:T(8,128)(4,1)S(1)} %fusion.58, bf16[4,256,1,8,64]{1,4,3,2,0:T(8,128)(2,1)} %get-tuple-element.310, s32[]{:T(128)S(6)} %copy.74, bf16[256,1,2,64]{0,3,2,1:T(8,128)(2,1)S(1)} %dynamic-slice_bitcast_fusion.4, ...), kind=kOutput, calls=%fused_computation.10.clone.1 | convolution fusion | flops 618723328 | bytes 20324356 | tf_op jit(solution)/shard_map/while/body/eval_jaxpr/ckgd,tkd->kgct/dot_general | solution.py:40
  52.3 10.2 %fusion.60 = f32[8,256]{1,0:T(8,128)S(1)} fusion(f32[2304,256,8]{1,0,2:T(8,128)} %get-tuple-element.284, f32[8,256]{1,0:T(8,128)S(1)} %get-tuple-element.285, pred[256,2304]{0,1:T(8,128)(4,1)S(1)} %fusion.58), kind=kLoop, calls=%fused_computation.9.clone.1 | loop fusion | flops 18872320 | bytes 19480576 | tf_op jit(solution)/shard_map/while/body/eval_jaxpr/reduce_sum | solution.py:53
  62.4 9.0 %fusion.61 = bf16[64,8,256]{2,0,1:T(8,128)(2,1)S(1)} fusion(f32[8,256]{1,0:T(8,128)S(1)} %fusion.60, f32[8,256]{1,0:T(8,128)S(1)} %get-tuple-element.285, f32[2304,256,8]{1,0,2:T(8,128)} %get-tuple-element.284, pred[256,2304]{0,1:T(8,128)(4,1)S(1)} %fusion.58, bf16[2048,1,2,64]{0,3,2,1:T(8,128)(2,1)S(1)} %dynamic-slice_bitcast_fusion.5, ...), kind=kOutput, calls=%fused_computation.17.clone.1 | convolution fusion | flops 628293632 | bytes 20332544 | tf_op jit(solution)/shard_map/while/body/eval_jaxpr/kgct,tkd->ckgd/dot_general | solution.py:54
  73.8 1.3 dynamic_slice.91
  75.8 2.0 fusion.58
  77.9 1.1 dynamic-slice_bitcast_fusion.5
  78.9 9.0 %fusion.59 = (f32[8,256]{1,0:T(8,128)S(1)}, f32[2304,256,8]{1,0,2:T(8,128)}) fusion(pred[256,2304]{0,1:T(8,128)(4,1)S(1)} %fusion.58, bf16[4,256,1,8,64]{1,4,3,2,0:T(8,128)(2,1)} %get-tuple-element.310, s32[]{:T(128)S(6)} %copy.74, bf16[256,1,2,64]{0,3,2,1:T(8,128)(2,1)S(1)} %dynamic-slice_bitcast_fusion.4, ...), kind=kOutput, calls=%fused_computation.10.clone.1 | convolution fusion | flops 618723328 | bytes 20324356 | tf_op jit(solution)/shard_map/while/body/eval_jaxpr/ckgd,tkd->kgct/dot_general | solution.py:40
  87.9 10.2 %fusion.60 = f32[8,256]{1,0:T(8,128)S(1)} fusion(f32[2304,256,8]{1,0,2:T(8,128)} %get-tuple-element.284, f32[8,256]{1,0:T(8,128)S(1)} %get-tuple-element.285, pred[256,2304]{0,1:T(8,128)(4,1)S(1)} %fusion.58), kind=kLoop, calls=%fused_computation.9.clone.1 | loop fusion | flops 18872320 | bytes 19480576 | tf_op jit(solution)/shard_map/while/body/eval_jaxpr/reduce_sum | solution.py:53
  98.1 9.0 %fusion.61 = bf16[64,8,256]{2,0,1:T(8,128)(2,1)S(1)} fusion(f32[8,256]{1,0:T(8,128)S(1)} %fusion.60, f32[8,256]{1,0:T(8,128)S(1)} %get-tuple-element.285, f32[2304,256,8]{1,0,2:T(8,128)} %get-tuple-element.284, pred[256,2304]{0,1:T(8,128)(4,1)S(1)} %fusion.58, bf16[2048,1,2,64]{0,3,2,1:T(8,128)(2,1)S(1)} %dynamic-slice_bitcast_fusion.5, ...), kind=kOutput, calls=%fused_computation.17.clone.1 | convolution fusion | flops 628293632 | bytes 20332544 | tf_op jit(solution)/shard_map/while/body/eval_jaxpr/kgct,tkd->ckgd/dot_general | solution.py:54
  109.5 1.3 dynamic_slice.91
  111.4 2.0 fusion.58
  113.5 1.1 dynamic-slice_bitcast_fusion.5
  114.6 9.0 %fusion.59 = (f32[8,256]{1,0:T(8,128)S(1)}, f32[2304,256,8]{1,0,2:T(8,128)}) fusion(pred[256,2304]{0,1:T(8,128)(4,1)S(1)} %fusion.58, bf16[4,256,1,8,64]{1,4,3,2,0:T(8,128)(2,1)} %get-tuple-element.310, s32[]{:T(128)S(6)} %copy.74, bf16[256,1,2,64]{0,3,2,1:T(8,128)(2,1)S(1)} %dynamic-slice_bitcast_fusion.4, ...), kind=kOutput, calls=%fused_computation.10.clone.1 | convolution fusion | flops 618723328 | bytes 20324356 | tf_op jit(solution)/shard_map/while/body/eval_jaxpr/ckgd,tkd->kgct/dot_general | solution.py:40
  123.6 10.2 %fusion.60 = f32[8,256]{1,0:T(8,128)S(1)} fusion(f32[2304,256,8]{1,0,2:T(8,128)} %get-tuple-element.284, f32[8,256]{1,0:T(8,128)S(1)} %get-tuple-element.285, pred[256,2304]{0,1:T(8,128)(4,1)S(1)} %fusion.58), kind=kLoop, calls=%fused_computation.9.clone.1 | loop fusion | flops 18872320 | bytes 19480576 | tf_op jit(solution)/shard_map/while/body/eval_jaxpr/reduce_sum | solution.py:53
  133.8 9.0 %fusion.61 = bf16[64,8,256]{2,0,1:T(8,128)(2,1)S(1)} fusion(f32[8,256]{1,0:T(8,128)S(1)} %fusion.60, f32[8,256]{1,0:T(8,128)S(1)} %get-tuple-element.285, f32[2304,256,8]{1,0,2:T(8,128)} %get-tuple-element.284, pred[256,2304]{0,1:T(8,128)(4,1)S(1)} %fusion.58, bf16[2048,1,2,64]{0,3,2,1:T(8,128)(2,1)S(1)} %dynamic-slice_bitcast_fusion.5, ...), kind=kOutput, calls=%fused_computation.17.clone.1 | convolution fusion | flops 628293632 | bytes 20332544 | tf_op jit(solution)/shard_map/while/body/eval_jaxpr/kgct,tkd->ckgd/dot_general | solution.py:54
  145.1 1.3 dynamic_slice.91
  147.1 2.0 fusion.58
  149.2 1.1 dynamic-slice_bitcast_fusion.5
  150.2 9.0 %fusion.59 = (f32[8,256]{1,0:T(8,128)S(1)}, f32[2304,256,8]{1,0,2:T(8,128)}) fusion(pred[256,2304]{0,1:T(8,128)(4,1)S(1)} %fusion.58, bf16[4,256,1,8,64]{1,4,3,2,0:T(8,128)(2,1)} %get-tuple-element.310, s32[]{:T(128)S(6)} %copy.74, bf16[256,1,2,64]{0,3,2,1:T(8,128)(2,1)S(1)} %dynamic-slice_bitcast_fusion.4, ...), kind=kOutput, calls=%fused_computation.10.clone.1 | convolution fusion | flops 618723328 | bytes 20324356 | tf_op jit(solution)/shard_map/while/body/eval_jaxpr/ckgd,tkd->kgct/dot_general | solution.py:40
  159.2 10.2 %fusion.60 = f32[8,256]{1,0:T(8,128)S(1)} fusion(f32[2304,256,8]{1,0,2:T(8,128)} %get-tuple-element.284, f32[8,256]{1,0:T(8,128)S(1)} %get-tuple-element.285, pred[256,2304]{0,1:T(8,128)(4,1)S(1)} %fusion.58), kind=kLoop, calls=%fused_computation.9.clone.1 | loop fusion | flops 18872320 | bytes 19480576 | tf_op jit(solution)/shard_map/while/body/eval_jaxpr/reduce_sum | solution.py:53
  169.4 9.0 %fusion.61 = bf16[64,8,256]{2,0,1:T(8,128)(2,1)S(1)} fusion(f32[8,256]{1,0:T(8,128)S(1)} %fusion.60, f32[8,256]{1,0:T(8,128)S(1)} %get-tuple-element.285, f32[2304,256,8]{1,0,2:T(8,128)} %get-tuple-element.284, pred[256,2304]{0,1:T(8,128)(4,1)S(1)} %fusion.58, bf16[2048,1,2,64]{0,3,2,1:T(8,128)(2,1)S(1)} %dynamic-slice_bitcast_fusion.5, ...), kind=kOutput, calls=%fused_computation.17.clone.1 | convolution fusion | flops 628293632 | bytes 20332544 | tf_op jit(solution)/shard_map/while/body/eval_jaxpr/kgct,tkd->ckgd/dot_general | solution.py:54
  180.8 6.8 %fusion.45 = f32[1024,2048]{1,0:T(8,128)} fusion(bf16[1024,512]{1,0:T(8,128)(2,1)} %bitcast.102, bf16[512,2048]{1,0:T(8,128)(2,1)S(1)} %copy-done), kind=kOutput, calls=%fused_computation.92 | convolution fusion | flops 2147483648 | bytes 11534336 | tf_op jit(solution)/shard_map/dot_general | solution.py:65
  187.8 7.9 %all-gather = s32[8,4,2]{1,2,0:T(2,128)S(1)} all-gather(s32[1,4,2]{1,2,0:T(2,128)S(1)} %bitcast.100), channel_id=1, replica_groups=mesh['group'=4,'dp'=2,'tensor'=4] {'group','dp'}, dimensions={0}, use_global_device_ids=true | all-gather | bytes 288 | tf_op jit(solution)/shard_map/all_gather | solution.py:81
  196.5 1.0 scatter_custom_fusion.1
  197.6 6.5 %gather_fusion = bf16[32,4,128,128]{3,2,1,0:T(8,128)(2,1)} fusion(bf16[4,64,128,128]{3,2,1,0:T(8,128)(2,1)} %bitcast.99, s32[1024]{0:T(1024)S(1)} %pad_clamp_fusion.1), kind=kCustom, calls=%fused_computation | custom fusion | bytes 8388736 | tf_op jit(solution)/shard_map/jit(_take)/gather | solution.py:95
  204.0 4.7 %select_bitcast_fusion.1 = bf16[4,32,128,128]{3,2,0,1:T(8,128)(2,1)} fusion(bf16[32,4,128,128]{3,2,1,0:T(8,128)(2,1)} %gather_fusion, pred[32]{0:T(512)(128)(4,1)S(1)} %compare_and_fusion), kind=kLoop, calls=%fused_computation.48 | loop fusion | flops 2097152 | bytes 8388640 | tf_op jit(solution)/shard_map/jit(_take)/select_n | solution.py:95
  208.7 6.0 %all-to-all-start = ((bf16[4,32,128,128]{3,2,0,1:T(8,128)(2,1)}), bf16[4,32,128,128]{3,2,0,1:T(8,128)(2,1)}, u32[]{:S(2)}, u32[]{:S(2)}) async-start(bf16[4,32,128,128]{3,2,0,1:T(8,128)(2,1)} %select_bitcast_fusion.1), calls=%async_computation.1 | async-start | bytes 8388608 | tf_op jit(solution)/shard_map/all_to_all | solution.py:96
  215.1 2.4 scatter_custom_fusion
  217.6 44.0 %all-to-all-done = bf16[4,32,128,128]{3,2,0,1:T(8,128)(2,1)} async-done(((bf16[4,32,128,128]{3,2,0,1:T(8,128)(2,1)}), bf16[4,32,128,128]{3,2,0,1:T(8,128)(2,1)}, u32[]{:S(2)}, u32[]{:S(2)}) %all-to-all-start) | async-done | bytes 4194336 | tf_op jit(solution)/shard_map/all_to_all | solution.py:96
  261.6 4.7 %copy.60 = bf16[4,32,128,128]{3,2,1,0:T(8,128)(2,1)} copy(bf16[4,32,128,128]{3,2,0,1:T(8,128)(2,1)} %all-to-all-done) | data formatting | bytes 8388608 | tf_op jit(solution)/shard_map/all_to_all | solution.py:96
  266.3 7.8 %gather_fusion.1 = bf16[64,4,128,128]{3,2,1,0:T(8,128)(2,1)} fusion(bf16[4,32,128,128]{3,2,1,0:T(8,128)(2,1)} %copy.60, s32[1024]{0:T(1024)S(1)} %pad_clamp_fusion), kind=kCustom, calls=%fused_computation.1 | custom fusion | bytes 16777472 | tf_op jit(solution)/shard_map/jit(_take)/gather | solution.py:105
  274.2 7.2 %select_bitcast_fusion = bf16[4,64,128,128]{3,2,0,1:T(8,128)(2,1)} fusion(bf16[64,4,128,128]{3,2,1,0:T(8,128)(2,1)} %gather_fusion.1, pred[64]{0:T(512)(128)(4,1)S(1)} %compare_and_fusion.1), kind=kLoop, calls=%fused_computation.47 | loop fusion | flops 4194304 | bytes 16777280 | tf_op jit(solution)/shard_map/jit(_take)/select_n | solution.py:105
  281.4 10.6 %copy.61 = bf16[4,64,128,128]{3,2,1,0:T(8,128)(2,1)} copy(bf16[4,64,128,128]{3,2,0,1:T(8,128)(2,1)} %select_bitcast_fusion) | data formatting | bytes 16777216
  292.0 41.4 %reduce-scatter.2.cloned.1.call-done = f32[256,2048]{1,0:T(8,128)} async-done(((f32[1024,2048]{1,0:T(8,128)}), f32[256,2048]{1,0:T(8,128)}) %reduce-scatter.2.cloned.1.call-update) | async-done | bytes 2097168 | tf_op jit(solution)/shard_map/reduce_scatter | solution.py:64
  333.4 2.7 convert_element_type.44
  (90 shorter events, 11.3 us)
Async XLA Ops:
  7.2 173.6 %copy-start = (bf16[512,2048]{1,0:T(8,128)(2,1)S(1)}, bf16[512,2048]{1,0:T(8,128)(2,1)}, u32[]{:S(2)}) copy-start(bf16[512,2048]{1,0:T(8,128)(2,1)} %param.14) | copy-start | bytes 6291460
  7.2 13.2 %copy-start.2 = (bf16[2048]{0:T(1024)(128)(2,1)S(1)}, bf16[2048]{0:T(1024)(128)(2,1)}, u32[]{:S(2)}) copy-start(bf16[2048]{0:T(1024)(128)(2,1)} %param.11) | copy-start | bytes 12292
  7.2 326.2 %reduce-scatter.2.cloned.1.call-start = ((), (), s32[]{:S(2)}) async-start(), calls=%async_computation.2 | async-start | bytes 10485760 | tf_op jit(solution)/shard_map/reduce_scatter | solution.py:64
  62.4 9.1 %copy-start.4 = (s32[4]{0:T(128)S(1)}, s32[4]{0:T(128)}, u32[]{:S(2)}) copy-start(s32[4]{0:T(128)} %get-tuple-element.306) | copy-start | bytes 52 | tf_op jit(solution)/shard_map/while
  98.1 9.1 %copy-start.4 = (s32[4]{0:T(128)S(1)}, s32[4]{0:T(128)}, u32[]{:S(2)}) copy-start(s32[4]{0:T(128)} %get-tuple-element.306) | copy-start | bytes 52 | tf_op jit(solution)/shard_map/while
  133.7 9.1 %copy-start.4 = (s32[4]{0:T(128)S(1)}, s32[4]{0:T(128)}, u32[]{:S(2)}) copy-start(s32[4]{0:T(128)} %get-tuple-element.306) | copy-start | bytes 52 | tf_op jit(solution)/shard_map/while
  169.4 9.1 %copy-start.4 = (s32[4]{0:T(128)S(1)}, s32[4]{0:T(128)}, u32[]{:S(2)}) copy-start(s32[4]{0:T(128)} %get-tuple-element.306) | copy-start | bytes 52 | tf_op jit(solution)/shard_map/while
  180.8 6.8 %copy-start.1 = (s32[32,16]{0,1:T(8,128)S(1)}, s32[32,16]{0,1:T(8,128)}, u32[]{:S(2)}) copy-start(s32[32,16]{0,1:T(8,128)} %param.17) | copy-start | bytes 6148
  180.8 7.0 %copy-start.3 = (s32[4,2]{0,1:T(2,128)S(1)}, s32[4,2]{0,1:T(2,128)}, u32[]{:S(2)}) copy-start(s32[4,2]{0,1:T(2,128)} %param.16) | copy-start | bytes 100
  208.7 52.8 %all-to-all-start = ((bf16[4,32,128,128]{3,2,0,1:T(8,128)(2,1)}), bf16[4,32,128,128]{3,2,0,1:T(8,128)(2,1)}, u32[]{:S(2)}, u32[]{:S(2)}) async-start(bf16[4,32,128,128]{3,2,0,1:T(8,128)(2,1)} %select_bitcast_fusion.1), calls=%async_computation.1 | async-start | bytes 8388608 | tf_op jit(solution)/shard_map/all_to_all | solution.py:96
Sparse Core Ops, SparseCore 0:
  187.7 145.6 reduce-scatter.1
where the time goes:
time: 346 us; the launch traced here: 343 us
  matrix products  87.7 us (25%)
  waiting for transfers between devices  85.4 us (25%)
  other arithmetic  70.1 us (20%)
  local copies, waits for them, and re-layouts  68.5 us (20%)
  between operations  14.2 us (4%)
  blocking collectives  7.9 us (2%)
  starting transfers between devices  6 us (2%)
    all_to_all x1, waiting for transfers between devices, per_device(): lax.all_to_all(outgoing, ('group', 'dp'), split_axis=1, concat_axis=1, ti...  44 us
    reduce_scatter x1, waiting for transfers between devices, per_device(): lax.psum_scatter(jnp.dot(attn, w_out, preferred_element_type=jnp.float32)...  41.4 us
    reduce_sum x4, other arithmetic, attend(): jnp.sum(expo, axis=-1, keepdims=True)  40.7 us
    dot_general x4, matrix products, attend(): jnp.einsum('kgct,tkd->ckgd', weights, pairs[:, :, 1], preferred_element_t...  36.2 us
    dot_general x4, matrix products, attend(): jnp.einsum('ckgd,tkd->kgct', query_p, pairs[:, :, 0], preferred_element_t...  35.9 us
    unnamed x13, local copies, waits for them, and re-layouts  14.1 us
    select_n x4, other arithmetic, attend(): jnp.where(key_pos < window, (key_pos >= window - history) & (key_pos >= q...  8.15 us
    all_gather x1, blocking collectives, per_device(): lengths_every = lax.all_gather(lengths, ('group', 'dp'), axis=0, tiled=True)  7.9 us
  transfers between devices with their start and end apart: 2, of which 2 were waited for; matrix products, arithmetic and copies ran while one was open for 14% of the time, Pallas kernels for 0%

commit v1 on v0

v1 whole, which is shorter than its diff:
```python
import jax
import jax.numpy as jnp
from jax import lax
from jax.experimental import pallas as pl
from jax.experimental.pallas import tpu as pltpu
from jax.sharding import PartitionSpec as P

HD = 64
EPS = 1e-05
CHUNK = 256
NEG = -1e30
VMEM_LIMIT = 48 * 1024 * 1024


def project_kernel(tok_ref, gain_ref, wq_ref, wkv_ref, q_ref, kv_ref):
    x = tok_ref[...].astype(jnp.float32)
    inv = lax.rsqrt(jnp.mean(x * x, axis=-1, keepdims=True) + EPS)
    normed = (x * inv * gain_ref[...].astype(jnp.float32)).astype(jnp.bfloat16)
    kv_ref[...] = jnp.dot(normed, wkv_ref[...], preferred_element_type=jnp.float32).astype(
        jnp.bfloat16
    )
    q = jnp.dot(normed, wq_ref[...], preferred_element_type=jnp.float32) * (1.0 / HD**0.5)
    low = lax.broadcasted_iota(jnp.int32, (q.shape[0], 2 * HD), 1) < HD
    for pair in range(q.shape[1] // (2 * HD)):
        both = q[:, pair * 2 * HD : (pair + 1) * 2 * HD]
        q_ref[2 * pair] = jnp.where(low, both, 0.0).astype(jnp.bfloat16)
        q_ref[2 * pair + 1] = jnp.where(low, pltpu.roll(both, HD, 1), 0.0).astype(jnp.bfloat16)


def project(tokens, norm_gain, w_query, w_keyval, fresh_rows):
    rows, width = tokens.shape
    heads = w_query.shape[1] // HD
    return pl.pallas_call(
        project_kernel,
        grid=(rows // fresh_rows,),
        in_specs=[
            pl.BlockSpec((fresh_rows, width), lambda i: (i, 0)),
            pl.BlockSpec((1, width), lambda i: (0, 0)),
            pl.BlockSpec(w_query.shape, lambda i: (0, 0)),
            pl.BlockSpec(w_keyval.shape, lambda i: (0, 0)),
        ],
        out_specs=[
            pl.BlockSpec((heads, fresh_rows, 2 * HD), lambda i: (0, i, 0)),
            pl.BlockSpec((fresh_rows, 2 * HD), lambda i: (i, 0)),
        ],
        out_shape=[
            jax.ShapeDtypeStruct((heads, rows, 2 * HD), jnp.bfloat16),
            jax.ShapeDtypeStruct((rows, 2 * HD), jnp.bfloat16),
        ],
        compiler_params=pltpu.CompilerParams(vmem_limit_bytes=VMEM_LIMIT),
        cost_estimate=pl.CostEstimate(
            flops=2 * rows * width * (heads + 2) * HD, bytes_accessed=10**7, transcendentals=0
        ),
        name="project",
    )(tokens, norm_gain.reshape(1, width), w_query, w_keyval)


def attend_kernel(info_ref, q_ref, kv_ref, cache_ref, out_ref, s_ref, m_ref, acc_ref):
    history, fresh = info_ref[1], info_ref[2]
    heads, rows, lanes = q_ref.shape
    window = cache_ref.shape[2] * cache_ref.shape[3]
    chunks = window // CHUNK
    blocks = CHUNK // cache_ref.shape[3]
    start = window - history
    first = start // CHUNK
    trans = (((1,), (1,)), ((), ()))

    def cached(c):
        return cache_ref[0, 0, pl.ds(c * blocks, blocks)].reshape(CHUNK, lanes)

    def score(h, keys):
        return lax.dot_general(q_ref[h], keys, trans, preferred_element_type=jnp.float32)

    row = lax.broadcasted_iota(jnp.int32, (rows, CHUNK), 0)
    col = lax.broadcasted_iota(jnp.int32, (rows, CHUNK), 1)
    new = kv_ref[...]

    def keep(h, c, s, begin):
        s_ref[c, h] = s
        best = jnp.maximum(s[:, :lanes], s[:, lanes:])
        m_ref[h] = best if begin else jnp.maximum(m_ref[h], best)

    causal = col <= row
    for h in range(heads):
        keep(h, chunks, jnp.where(causal, score(h, new), NEG), True)

    @pl.when(first < chunks)
    def _():
        at = first * CHUNK + col
        seen = (at >= start) & (at >= row + 1)
        keys = cached(first)
        for h in range(heads):
            keep(h, first, jnp.where(seen, score(h, keys), NEG), False)

    def scores(c, carry):
        keys = cached(c)
        for h in range(heads):
            keep(h, c, score(h, keys), False)
        return carry

    lax.fori_loop(first + 1, chunks, scores, 0)

    for h in range(heads):
        m_ref[h] = jnp.broadcast_to(jnp.max(m_ref[h], axis=1, keepdims=True), (rows, lanes))

    low_keys = lax.broadcasted_iota(jnp.int32, (CHUNK, lanes), 1) < HD

    def gather(c, pairs, begin):
        vals = jnp.where(low_keys, jnp.ones_like(pairs), pairs)
        for h in range(heads):
            s = s_ref[c, h]
            m = m_ref[h]
            p = jnp.exp(s - jnp.concatenate([m, m], axis=1)).astype(jnp.bfloat16)
            o = jnp.dot(p, vals, preferred_element_type=jnp.float32)
            acc_ref[h] = o if begin else acc_ref[h] + o

    gather(chunks, new, True)

    def weigh(c, carry):
        gather(c, cached(c), False)
        return carry

    lax.fori_loop(first, chunks, weigh, 0)

    low = lax.broadcasted_iota(jnp.int32, (rows, lanes), 1) < HD
    live = lax.broadcasted_iota(jnp.int32, (rows, lanes), 0) < fresh
    for pair in range(heads // 2):
        even, odd = acc_ref[2 * pair], acc_ref[2 * pair + 1]
        even = pltpu.roll(even, HD, 1) / even
        odd = odd / pltpu.roll(odd, HD, 1)
        both = jnp.where(live, jnp.where(low, even, odd), 0.0)
        out_ref[:, pair * lanes : (pair + 1) * lanes] = both.astype(jnp.bfloat16)


def attend(info, query, keyval, kv_cache):
    heads, rows_all, lanes = query.shape
    _, prompts, blocks, block_len, _ = kv_cache.shape
    rows = rows_all // prompts
    chunks = blocks * block_len // CHUNK
    return pl.pallas_call(
        attend_kernel,
        grid_spec=pltpu.PrefetchScalarGridSpec(
            num_scalar_prefetch=1,
            grid=(1,),
            in_specs=[
                pl.BlockSpec((heads, rows, lanes), lambda i, info: (0, info[0], 0)),
                pl.BlockSpec((rows, lanes), lambda i, info: (info[0], 0)),
                pl.BlockSpec(
                    (1, 1, blocks, block_len, lanes), lambda i, info: (0, info[0], 0, 0, 0)
                ),
            ],
            out_specs=pl.BlockSpec((rows, heads * HD), lambda i, info: (0, 0)),
            scratch_shapes=[
                pltpu.VMEM((chunks + 1, heads, rows, CHUNK), jnp.float32),
                pltpu.VMEM((heads, rows, lanes), jnp.float32),
                pltpu.VMEM((heads, rows, lanes), jnp.float32),
            ],
        ),
        out_shape=jax.ShapeDtypeStruct((rows, heads * HD), jnp.bfloat16),
        compiler_params=pltpu.CompilerParams(vmem_limit_bytes=VMEM_LIMIT),
        cost_estimate=pl.CostEstimate(
            flops=10**9, bytes_accessed=10**6, transcendentals=0
        ),
        name="attend",
    )(info, query, keyval, kv_cache)


def pick_kernel(me_ref, dest_ref, len_ref, cache_ref, out_ref, count_ref, sems):
    per_dev = cache_ref.shape[1]
    total = out_ref.shape[0]
    blocks = per_dev // len_ref.shape[0]
    block_len = cache_ref.shape[2]
    window = blocks * block_len
    devices = count_ref.shape[0]
    capacity = total // devices
    base = me_ref[0] * per_dev
    for d in range(devices):
        count_ref[d] = 0

    def send(j, carry):
        p, b = j // blocks, j % blocks

        @pl.when((b + 1) * block_len > window - len_ref[p, 0])
        def _():
            peer = dest_ref[base + j] // per_dev
            at = peer * capacity + count_ref[peer]
            count_ref[peer] = count_ref[peer] + 1
            pltpu.make_async_copy(cache_ref.at[:, j], out_ref.at[at], sems.at[at]).start()

        return carry

    lax.fori_loop(0, per_dev, send, 0)

    def done(j, carry):
        pltpu.make_async_copy(cache_ref.at[:, 0], out_ref.at[j], sems.at[j]).wait()
        return carry

    lax.fori_loop(0, total, done, 0)


def place_kernel(src_ref, in_ref, out_ref, zero_ref, sems):
    zero_ref[...] = jnp.zeros_like(zero_ref)
    slots = out_ref.shape[1]

    def send(j, carry):
        src = src_ref[j]

        @pl.when(src >= 0)
        def _():
            pltpu.make_async_copy(in_ref.at[src], out_ref.at[:, j], sems.at[j]).start()

        @pl.when(src < 0)
        def _():
            pltpu.make_async_copy(zero_ref, out_ref.at[:, j], sems.at[j]).start()

        return carry

    lax.fori_loop(0, slots, send, 0)

    def done(j, carry):
        pltpu.make_async_copy(zero_ref, out_ref.at[:, j], sems.at[j]).wait()
        return carry

    lax.fori_loop(0, slots, done, 0)


def mix_kernel(a_ref, b_ref, c_ref, d_ref, order_ref, w_ref, out_ref):
    halves, shards, depth, _ = w_ref.shape
    total = None
    for ref, k in ((a_ref, 0), (b_ref, 1), (c_ref, 2), (d_ref, 3)):
        t = order_ref[k]
        for half in range(halves):
            term = jnp.dot(
                ref[:, half * depth : (half + 1) * depth],
                w_ref[half, t],
                preferred_element_type=jnp.float32,
            )
            total = term if total is None else total + term
    out_ref[...] = total.astype(jnp.bfloat16)


def mix(parts, order, w_all):
    rows, depth = parts[0].shape
    halves, shards, half_depth, width = w_all.shape
    tile = 512
    part = pl.BlockSpec((rows, depth), lambda i: (0, 0))
    return pl.pallas_call(
        mix_kernel,
        grid=(width // tile,),
        in_specs=[part] * len(parts)
        + [
            pl.BlockSpec(memory_space=pltpu.SMEM),
            pl.BlockSpec((halves, shards, half_depth, tile), lambda i: (0, 0, 0, i)),
        ],
        out_specs=pl.BlockSpec((rows, tile), lambda i: (0, i)),
        out_shape=jax.ShapeDtypeStruct((rows, width), jnp.bfloat16),
        compiler_params=pltpu.CompilerParams(vmem_limit_bytes=VMEM_LIMIT),
        cost_estimate=pl.CostEstimate(
            flops=2 * rows * depth * 4 * width, bytes_accessed=10**7, transcendentals=0
        ),
        name="mix",
    )(*parts, order, w_all)


def per_device(tokens, norm_gain, w_query, w_keyval, w_out, kv_cache, lengths, dest_slot):
    prompts = lengths.shape[0]
    fresh_rows = tokens.shape[0] // prompts
    layers, _, blocks_win, block_len, lane_width = kv_cache.shape
    window = blocks_win * block_len
    per_dev = prompts * blocks_win
    devices = lax.axis_size(("group", "dp"))
    capacity = per_dev // devices // 2
    total = devices * capacity
    me = lax.axis_index(("group", "dp")).astype(jnp.int32)
    dest_flat = dest_slot.reshape(-1)
    raw = kv_cache.reshape(layers, per_dev, block_len, lane_width)

    smem = pl.BlockSpec(memory_space=pltpu.SMEM)
    hbm = pl.BlockSpec(memory_space=pltpu.HBM)
    outgoing = pl.pallas_call(
        pick_kernel,
        in_specs=[smem, smem, smem, hbm],
        out_specs=hbm,
        out_shape=jax.ShapeDtypeStruct((total, layers, block_len, lane_width), jnp.bfloat16),
        scratch_shapes=[pltpu.SMEM((devices,), jnp.int32), pltpu.SemaphoreType.DMA((total,))],
        cost_estimate=pl.CostEstimate(flops=0, bytes_accessed=10**7, transcendentals=0),
        name="pick",
    )(me.reshape(1), dest_flat, lengths, raw)
    flat = jnp.zeros((8 * 128,), jnp.float32).at[: lengths.size].set(
        lengths.reshape(-1).astype(jnp.float32)
    )
    tiles = lax.all_gather(flat.reshape(8, 128), ("group", "dp"), axis=0)
    norm_gain, outgoing = lax.optimization_barrier((norm_gain, outgoing))
    incoming = lax.all_to_all(outgoing, ("group", "dp"), split_axis=0, concat_axis=0, tiled=True)

    cores = lax.axis_size("dp")
    depth = w_out.shape[0] // cores
    half = lax.dynamic_slice_in_dim(w_out, lax.axis_index("dp") * depth, depth, 0)
    w_all = lax.all_gather(half, ("dp", "tensor"), axis=0).reshape(cores, -1, *half.shape)

    query, keyval = project(tokens, norm_gain, w_query, w_keyval, fresh_rows)
    t_size = lax.axis_size("tensor")
    t = lax.axis_index("tensor").astype(jnp.int32)
    parts, order = [], []

    def shift(by):
        return [(i, (i + by) % t_size) for i in range(t_size)]

    for step in range(1, t_size + 1):
        p = (t + step) % t_size
        own = lax.dynamic_index_in_dim(lengths, p, 0, keepdims=False)
        info = jnp.concatenate([p.reshape(1), own])
        if step > 1:
            info = lax.optimization_barrier((info, part))[0]
        part = attend(info, query, keyval, kv_cache)
        parts.append(lax.ppermute(part, "tensor", shift(step)) if step < t_size else part)
        order.append((t - step + t_size) % t_size)
    mixed = mix(parts, jnp.stack(order), w_all)

    lengths_every = tiles.reshape(devices, -1)[:, : lengths.size].reshape(devices * prompts, -1)
    lengths_every = lengths_every.astype(jnp.int32)
    dest_all = dest_slot.reshape(devices, per_dev)
    recv_all = dest_all // per_dev
    live_all = (
        (jnp.arange(blocks_win)[None, :] + 1) * block_len > window - lengths_every[:, 0:1]
    ).reshape(devices, per_dev)
    same = recv_all[:, :, None] == recv_all[:, None, :]
    earlier = jnp.arange(per_dev)[None, :] < jnp.arange(per_dev)[:, None]
    rank = jnp.sum(same & earlier[None] & live_all[:, None, :], axis=2, dtype=jnp.int32)
    where_from = jnp.arange(devices, dtype=jnp.int32)[:, None] * capacity + rank
    slot = jnp.where((recv_all == me) & live_all, dest_all - me * per_dev, -1)
    hit = slot.reshape(1, -1) == jnp.arange(per_dev, dtype=jnp.int32)[:, None]
    source = jnp.max(jnp.where(hit, where_from.reshape(1, -1), -1), axis=1)
    decode_cache = pl.pallas_call(
        place_kernel,
        in_specs=[smem, hbm],
        out_specs=hbm,
        out_shape=jax.ShapeDtypeStruct((layers, per_dev, block_len, lane_width), jnp.bfloat16),
        scratch_shapes=[
            pltpu.VMEM((layers, block_len, lane_width), jnp.bfloat16),
            pltpu.SemaphoreType.DMA((per_dev,)),
        ],
        cost_estimate=pl.CostEstimate(flops=0, bytes_accessed=10**7, transcendentals=0),
        name="place",
    )(*lax.optimization_barrier((source, incoming, part))[:2])
    return (mixed, decode_cache)


def solution(mesh):
    in_specs = (
        P(("group", "dp"), None),
        P(),
        P(None, "tensor"),
        P(None, "tensor"),
        P("tensor", None),
        P(None, ("group", "dp"), None, None, "tensor"),
        P(("group", "dp"), None),
        P(),
    )
    out_specs = (P(("group", "dp", "tensor"), None), P(None, ("group", "dp"), None, "tensor"))
    return jax.shard_map(
        per_device, mesh=mesh, in_specs=in_specs, out_specs=out_specs, check_vma=False
    )
```

time: 346 us -> 357 us (1.032)
  Pallas kernels: 0 us -> 298 us
  matrix products: 87.7 us -> 0 us
  waiting for transfers between devices: 85.4 us -> 0.05 us
  other arithmetic: 70.1 us -> 1.53 us
  local copies, waits for them, and re-layouts: 68.5 us -> 9.76 us
  starting transfers between devices: 6 us -> 14.1 us
  blocking collectives: 7.9 us -> 14.6 us
    pallas_call x0 -> x8, Pallas kernels: none -> 298 us  [the longest x1 129 us: per_device(): pl.pallas_call(place_kernel, in_specs=[smem, hbm], out_specs=hbm, out_sha...]
    dot_general x11 -> x0, matrix products: 87.7 us -> none  [the longest x4 36.2 us: attend(): jnp.einsum('kgct,tkd->ckgd', weights, pairs[:, :, 1], preferred_element_t...]
    all_to_all x1, waiting for transfers between devices: 44 us -> 0.01 us  [per_device(): lax.all_to_all(outgoing, ('group', 'dp'), split_axis=0, concat_axis=0, ti...]
    reduce_sum x6 -> x1, other arithmetic: 44.1 us -> 0.32 us  [per_device(): jnp.sum(same & earlier[None] & live_all[:, None, :], axis=2, dtype=jnp.in...]
    reduce_scatter x1 -> x0, waiting for transfers between devices: 41.4 us -> none  [per_device(): lax.psum_scatter(jnp.dot(attn, w_out, preferred_element_type=jnp.float32)...]
    select_n x14 -> x1, other arithmetic: 20.3 us -> 0.01 us  [per_device(): slot = jnp.where((recv_all == me) & live_all, dest_all - me * per_dev, -1)]
    gather x2 -> x0, local copies, waits for them, and re-layouts: 14.3 us -> none  [the longest x1 7.84 us: per_device(): jnp.take(incoming, source_idx, axis=1, mode='fill', fill_value=0)]
    ppermute x0 -> x3, starting transfers between devices: none -> 9.44 us  [per_device(): lax.ppermute(part, 'tensor', shift(step))]
  transfers between devices with their start and end apart: 2 -> 5, of which waited for: 2 -> 0; matrix products, arithmetic and copies ran while one was open for 14% -> 2% of each run, Pallas kernels for 0% -> 83%
where the time goes in v1:
time: 357 us; the launch traced here: 353 us
  Pallas kernels  298 us (83%)
  blocking collectives  14.6 us (4%)
  between operations  14.4 us (4%)
  starting transfers between devices  14.1 us (4%)
  local copies, waits for them, and re-layouts  9.76 us (3%)
    pallas_call x1, Pallas kernels, per_device(): pl.pallas_call(place_kernel, in_specs=[smem, hbm], out_specs=hbm, out_sha...  129 us
    pallas_call x1, Pallas kernels, per_device(): pl.pallas_call(pick_kernel, in_specs=[smem, smem, smem, hbm], out_specs=h...  129 us
    pallas_call x4, Pallas kernels, attend(): pl.pallas_call(attend_kernel, grid_spec=pltpu.PrefetchScalarGridSpec(num_...  26.3 us
    all_gather x1, blocking collectives, per_device(): tiles = lax.all_gather(flat.reshape(8, 128), ('group', 'dp'), axis=0)  14.6 us
    ppermute x3, starting transfers between devices, per_device(): lax.ppermute(part, 'tensor', shift(step))  9.44 us
  transfers between devices with their start and end apart: 5, of which 0 were waited for; matrix products, arithmetic and copies ran while one was open for 2% of the time, Pallas kernels for 83%

profile of v1, /device:TPU:6, one launch (start us, length us, event | category | flops | bytes accessed | tf_op | source)
XLA Modules:
  0.0 352.5 jit_solution(18157265208946653706)
XLA Ops:
  7.2 0.0 copy-start
  7.2 0.0 all-gather.3.cloned.1.call-start
  7.2 1.5 copy-done
  8.8 1.1 constant_dynamic-slice_fusion
  9.8 0.0 all-gather.3.cloned.1.call-update
  9.9 0.8 copy.20
  10.6 0.7 reshape.227.dest_ref
  11.3 1.3 copy.21.len_ref
  12.7 129.3 %pick.1 = bf16[32,4,128,128]{3,2,1,0:T(8,128)(2,1)} custom-call(s32[1]{0:T(128)} %bitcast.1.me_ref, s32[512]{0:T(512)} %reshape.227.dest_ref, s32[4,2]{1,0:T(4,128)} %copy.21.len_ref, bf16[4,64,128,128]{3,2,1,0:T(8,128)(2,1)} %bitcast.14), custom_call_target="tpu_custom_call" | custom-call | bytes 10000000 | tf_op jit(solution)/shard_map/pick/pallas_call | solution.py:280
  142.0 0.0 copy-start.7
  142.0 0.0 copy-start.5
  142.0 0.0 copy-start.4
  142.0 4.6 %all-to-all-start = ((bf16[32,4,128,128]{3,2,1,0:T(8,128)(2,1)}), bf16[32,4,128,128]{3,2,1,0:T(8,128)(2,1)}, u32[]{:S(2)}, u32[]{:S(2)}) async-start(bf16[32,4,128,128]{3,2,1,0:T(8,128)(2,1)} %pick.1), calls=%async_computation | async-start | bytes 8388608 | tf_op jit(solution)/shard_map/all_to_all | solution.py:294
  146.8 0.2 fusion.9
  147.0 0.1 pad_add_fusion.info_ref
  147.1 1.6 copy-done.3
  148.7 6.6 %project.1 = (bf16[8,1024,128]{2,1,0:T(8,128)(2,1)S(1)}, bf16[1024,128]{1,0:T(8,128)(2,1)S(1)}) custom-call(bf16[1024,2048]{1,0:T(8,128)(2,1)} %tok_ref.1, bf16[1,2048]{1,0:T(2,128)(2,1)S(1)} %reshape.229.gain_ref, bf16[2048,512]{1,0:T(8,128)(2,1)S(1)} %copy-done.3, bf16[2048,128]{1,0:T(8,128)(2,1)S(1)} %copy-done.4), custom_call_target="tpu_custom_call" | custom-call | flops 2684354560 | bytes 10000000 | tf_op jit(solution)/shard_map/project/pallas_call | solution.py:33
  155.3 4.9 %attend.4 = bf16[256,512]{1,0:T(8,128)(2,1)S(1)} custom-call(s32[3]{0:T(128)S(1)} %pad_add_fusion.info_ref, bf16[8,1024,128]{2,1,0:T(8,128)(2,1)S(1)} %get-tuple-element.24.q_ref, bf16[1024,128]{1,0:T(8,128)(2,1)S(1)} %get-tuple-element.25.kv_ref, bf16[4,4,16,128,128]{4,3,2,1,0:T(8,128)(2,1)} %cache_ref.7), custom_call_target="tpu_custom_call" | custom-call | flops 1000000000 | bytes 1000000 | tf_op jit(solution)/shard_map/attend/pallas_call | solution.py:140
  160.2 4.9 %collective-permute-start = (bf16[256,512]{1,0:T(8,128)(2,1)S(1)}, bf16[256,512]{1,0:T(8,128)(2,1)}, u32[]{:S(2)}, u32[]{:S(2)}) collective-permute-start(bf16[256,512]{1,0:T(8,128)(2,1)S(1)} %attend.4), channel_id=1, source_target_pairs={{0,1},{1,2},{2,3},{3,0},{4,5},{5,6},{6,7},{7,4},{8,9},{9,10},{10,1... | collective-permute-start | bytes 786440 | tf_op jit(solution)/shard_map/ppermute | solution.py:316
  165.1 0.1 pad_add_fusion.1
  165.2 7.4 %attend.5 = bf16[256,512]{1,0:T(8,128)(2,1)S(1)} custom-call(s32[3]{0:T(128)S(1)} %get-tuple-element.26.info_ref, bf16[8,1024,128]{2,1,0:T(8,128)(2,1)S(1)} %get-tuple-element.24.q_ref, bf16[1024,128]{1,0:T(8,128)(2,1)S(1)} %get-tuple-element.25.kv_ref, bf16[4,4,16,128,128]{4,3,2,1,0:T(8,128)(2,1)} %cache_ref.7), custom_call_target="tpu_custom_call" | custom-call | flops 1000000000 | bytes 1000000 | tf_op jit(solution)/shard_map/attend/pallas_call | solution.py:140
  172.6 4.5 %collective-permute-start.1 = (bf16[256,512]{1,0:T(8,128)(2,1)S(1)}, bf16[256,512]{1,0:T(8,128)(2,1)}, u32[]{:S(2)}, u32[]{:S(2)}) collective-permute-start(bf16[256,512]{1,0:T(8,128)(2,1)S(1)} %attend.5), channel_id=1, source_target_pairs={{0,2},{1,3},{2,0},{3,1},{4,6},{5,7},{6,4},{7,5},{8,10},{9,11},{10,... | collective-permute-start | bytes 786440 | tf_op jit(solution)/shard_map/ppermute | solution.py:316
  177.1 5.6 %attend.6 = bf16[256,512]{1,0:T(8,128)(2,1)S(1)} custom-call(s32[3]{0:T(128)S(1)} %get-tuple-element.27.info_ref, bf16[8,1024,128]{2,1,0:T(8,128)(2,1)S(1)} %get-tuple-element.24.q_ref, bf16[1024,128]{1,0:T(8,128)(2,1)S(1)} %get-tuple-element.25.kv_ref, bf16[4,4,16,128,128]{4,3,2,1,0:T(8,128)(2,1)} %cache_ref.7), custom_call_target="tpu_custom_call" | custom-call | flops 1000000000 | bytes 1000000 | tf_op jit(solution)/shard_map/attend/pallas_call | solution.py:140
  182.7 0.1 collective-permute-start.2
  182.8 0.1 reshape.235
  182.9 0.1 copy.22
  183.0 0.1 convert_element_type.16
  183.1 14.6 %all_gather.11 = f32[8,8,128]{2,1,0:T(8,128)S(1)} all-gather(f32[1,8,128]{2,1,0:T(8,128)S(1)} %pad_bitcast_fusion), channel_id=1, replica_groups=mesh['group'=4,'dp'=2,'tensor'=4] {'group','dp'}, dimensions={0}, use_global_device_ids=true | all-gather | bytes 36864 | tf_op jit(solution)/shard_map/all_gather | solution.py:292
  197.6 0.1 convert_element_type.18
  197.7 0.1 fusion
  197.8 0.1 gt.46
  197.9 0.1 gt.47
  198.0 0.1 gt.50
  198.1 0.1 gt.48
  198.1 0.1 pad_add_fusion.3.info_ref
  198.2 0.1 gt.43
  198.3 0.1 gt.45
  198.5 0.3 convert_reduce_fusion
  198.8 0.1 broadcast_add_fusion
  198.9 1.6 copy-done.2
  200.5 8.3 %attend.7.d_ref = bf16[256,512]{1,0:T(8,128)(2,1)S(1)} custom-call(s32[3]{0:T(128)S(1)} %pad_add_fusion.3.info_ref, bf16[8,1024,128]{2,1,0:T(8,128)(2,1)S(1)} %copy-done.2, bf16[1024,128]{1,0:T(8,128)(2,1)S(1)} %get-tuple-element.25.kv_ref, bf16[4,4,16,128,128]{4,3,2,1,0:T(8,128)(2,1)} %cache_ref.7), custom_call_target="tpu_custom_call" | custom-call | flops 1000000000 | bytes 1000000 | tf_op jit(solution)/shard_map/attend/pallas_call | solution.py:140
  208.8 0.1 add.126
  208.9 0.1 pad_add_fusion.4.order_ref
  209.0 0.7 select_reduce_fusion.src_ref
  209.6 0.0 all-to-all-done.in_ref
  209.6 129.4 %place.1 = bf16[4,64,128,128]{3,2,1,0:T(8,128)(2,1)} custom-call(s32[64]{0:T(128)} %select_reduce_fusion.src_ref, bf16[32,4,128,128]{3,2,1,0:T(8,128)(2,1)} %all-to-all-done.in_ref), custom_call_target="tpu_custom_call" | custom-call | bytes 10000000 | tf_op jit(solution)/shard_map/place/pallas_call | solution.py:334
  339.1 0.0 all-gather.3.cloned.1.call-done
  339.1 6.5 %mix.1 = bf16[256,2048]{1,0:T(8,128)(2,1)} custom-call(bf16[256,512]{1,0:T(8,128)(2,1)} %collective-permute-done.a_ref, bf16[256,512]{1,0:T(8,128)(2,1)} %collective-permute-done.1.b_ref, bf16[256,512]{1,0:T(8,128)(2,1)} %collective-permute-done.2.c_ref, bf16[256,512]{1,0:T(8,128)(2,1)S(1)} %attend.7.d_ref, s32[4]{0:T(128)S(1)} %pad_add_fusion.4.order_ref, ...), custom_call_target="tpu_custom_call" | custom-call | flops 2147483648 | bytes 10000000 | tf_op jit(solution)/shard_map/mix/pallas_call | solution.py:247
  (25 shorter events, 0.1 us)
Async XLA Ops:
  7.2 1.6 copy-start
  7.2 331.9 %all-gather.3.cloned.1.call-start = ((), (), s32[]{:S(2)}) async-start(), calls=%async_computation.1 | async-start | bytes 9437184 | tf_op jit(solution)/shard_map/all_gather | solution.py:299
  142.0 4.7 %copy-start.7 = (bf16[2048]{0:T(1024)(128)(2,1)S(1)}, bf16[2048]{0:T(1024)(128)(2,1)}, u32[]{:S(2)}) copy-start(bf16[2048]{0:T(1024)(128)(2,1)} %param.11) | copy-start | bytes 12292
  142.0 4.8 %copy-start.5 = (s32[4,2]{0,1:T(2,128)S(1)}, s32[4,2]{0,1:T(2,128)}, u32[]{:S(2)}) copy-start(s32[4,2]{0,1:T(2,128)} %param.16) | copy-start | bytes 100
  142.0 5.1 %copy-start.4 = (bf16[2048,128]{1,0:T(8,128)(2,1)S(1)}, bf16[2048,128]{1,0:T(8,128)(2,1)}, u32[]{:S(2)}) copy-start(bf16[2048,128]{1,0:T(8,128)(2,1)} %wkv_ref.1) | copy-start | bytes 1572868
  142.0 67.6 %all-to-all-start = ((bf16[32,4,128,128]{3,2,1,0:T(8,128)(2,1)}), bf16[32,4,128,128]{3,2,1,0:T(8,128)(2,1)}, u32[]{:S(2)}, u32[]{:S(2)}) async-start(bf16[32,4,128,128]{3,2,1,0:T(8,128)(2,1)} %pick.1), calls=%async_computation | async-start | bytes 8388608 | tf_op jit(solution)/shard_map/all_to_all | solution.py:294
  147.1 1.6 copy-start.3
  155.3 21.8 %copy-start.1 = (bf16[8,1024,128]{2,1,0:T(8,128)(2,1)}, bf16[8,1024,128]{2,1,0:T(8,128)(2,1)S(1)}, u32[]{:S(2)}) copy-start(bf16[8,1024,128]{2,1,0:T(8,128)(2,1)S(1)} %get-tuple-element.24.q_ref) | copy-start | bytes 6291460
  160.2 178.9 %collective-permute-start = (bf16[256,512]{1,0:T(8,128)(2,1)S(1)}, bf16[256,512]{1,0:T(8,128)(2,1)}, u32[]{:S(2)}, u32[]{:S(2)}) collective-permute-start(bf16[256,512]{1,0:T(8,128)(2,1)S(1)} %attend.4), channel_id=1, source_target_pairs={{0,1},{1,2},{2,3},{3,0},{4,5},{5,6},{6,7},{7,4},{8,9},{9,10},{10,1... | collective-permute-start | bytes 786440 | tf_op jit(solution)/shard_map/ppermute | solution.py:316
  172.6 166.5 %collective-permute-start.1 = (bf16[256,512]{1,0:T(8,128)(2,1)S(1)}, bf16[256,512]{1,0:T(8,128)(2,1)}, u32[]{:S(2)}, u32[]{:S(2)}) collective-permute-start(bf16[256,512]{1,0:T(8,128)(2,1)S(1)} %attend.5), channel_id=1, source_target_pairs={{0,2},{1,3},{2,0},{3,1},{4,6},{5,7},{6,4},{7,5},{8,10},{9,11},{10,... | collective-permute-start | bytes 786440 | tf_op jit(solution)/shard_map/ppermute | solution.py:316
  177.1 21.7 %copy-start.6 = (s32[512]{0:T(512)S(1)}, s32[512]{0:T(512)}, u32[]{:S(2)}) copy-start(s32[512]{0:T(512)} %reshape.227.dest_ref) | copy-start | bytes 6148
  182.7 156.4 %collective-permute-start.2 = (bf16[256,512]{1,0:T(8,128)(2,1)S(1)}, bf16[256,512]{1,0:T(8,128)(2,1)}, u32[]{:S(2)}, u32[]{:S(2)}) collective-permute-start(bf16[256,512]{1,0:T(8,128)(2,1)S(1)} %attend.6), channel_id=1, source_target_pairs={{0,3},{1,0},{2,1},{3,2},{4,7},{5,4},{6,5},{7,6},{8,11},{9,8},{10,9... | collective-permute-start | bytes 786440 | tf_op jit(solution)/shard_map/ppermute | solution.py:316
  198.9 1.6 copy-start.2
Sparse Core Ops, SparseCore 0:
  10.2 83.2 all-gather.2

commit v2 on v1

--- a/solution.py
+++ b/solution.py
@@ -55,7 +55,7 @@
     )(tokens, norm_gain.reshape(1, width), w_query, w_keyval)
 
 
-def attend_kernel(info_ref, q_ref, kv_ref, cache_ref, out_ref, s_ref, m_ref, acc_ref):
+def attend_kernel(info_ref, q_ref, kv_ref, cache_ref, out_ref, s_ref, m_ref, l_ref, acc_ref):
     history, fresh = info_ref[1], info_ref[2]
     heads, rows, lanes = q_ref.shape
     window = cache_ref.shape[2] * cache_ref.shape[3]
@@ -103,16 +103,32 @@
     for h in range(heads):
         m_ref[h] = jnp.broadcast_to(jnp.max(m_ref[h], axis=1, keepdims=True), (rows, lanes))
 
-    low_keys = lax.broadcasted_iota(jnp.int32, (CHUNK, lanes), 1) < HD
+    def exps(c, begin):
+        for h in range(heads):
+            m = m_ref[h]
+            e = jnp.exp(s_ref[c, h] - jnp.concatenate([m, m], axis=1))
+            s_ref[c, h] = e
+            both = e[:, :lanes] + e[:, lanes:]
+            l_ref[h] = both if begin else l_ref[h] + both
 
     def gather(c, pairs, begin):
-        vals = jnp.where(low_keys, jnp.ones_like(pairs), pairs)
         for h in range(heads):
-            s = s_ref[c, h]
-            m = m_ref[h]
-            p = jnp.exp(s - jnp.concatenate([m, m], axis=1)).astype(jnp.bfloat16)
-            o = jnp.dot(p, vals, preferred_element_type=jnp.float32)
+            inv = l_ref[h]
+            w = (s_ref[c, h] * jnp.concatenate([inv, inv], axis=1)).astype(jnp.bfloat16)
+            o = jnp.dot(w, pairs, preferred_element_type=jnp.float32)
             acc_ref[h] = o if begin else acc_ref[h] + o
+
+    exps(chunks, True)
+
+    def exponentiate(c, carry):
+        exps(c, False)
+        return carry
+
+    lax.fori_loop(first, chunks, exponentiate, 0)
+
+    for h in range(heads):
+        total = jnp.sum(l_ref[h], axis=1, keepdims=True)
+        l_ref[h] = jnp.broadcast_to(1.0 / total, (rows, lanes))
 
     gather(chunks, new, True)
 
@@ -126,8 +142,7 @@
     live = lax.broadcasted_iota(jnp.int32, (rows, lanes), 0) < fresh
     for pair in range(heads // 2):
         even, odd = acc_ref[2 * pair], acc_ref[2 * pair + 1]
-        even = pltpu.roll(even, HD, 1) / even
-        odd = odd / pltpu.roll(odd, HD, 1)
+        even = pltpu.roll(even, HD, 1)
         both = jnp.where(live, jnp.where(low, even, odd), 0.0)
         out_ref[:, pair * lanes : (pair + 1) * lanes] = both.astype(jnp.bfloat16)
 
@@ -154,6 +169,7 @@
                 pltpu.VMEM((chunks + 1, heads, rows, CHUNK), jnp.float32),
                 pltpu.VMEM((heads, rows, lanes), jnp.float32),
                 pltpu.VMEM((heads, rows, lanes), jnp.float32),
+                pltpu.VMEM((heads, rows, lanes), jnp.float32),
             ],
         ),
         out_shape=jax.ShapeDtypeStruct((rows, heads * HD), jnp.bfloat16),
@@ -166,59 +182,90 @@
 
 
 def pick_kernel(me_ref, dest_ref, len_ref, cache_ref, out_ref, count_ref, sems):
-    per_dev = cache_ref.shape[1]
-    total = out_ref.shape[0]
+    layers, per_dev, block_len, lanes = cache_ref.shape
+    total, rows, _ = out_ref.shape
     blocks = per_dev // len_ref.shape[0]
-    block_len = cache_ref.shape[2]
     window = blocks * block_len
     devices = count_ref.shape[0]
     capacity = total // devices
     base = me_ref[0] * per_dev
+    tail = layers * block_len
     for d in range(devices):
         count_ref[d] = 0
 
+    def block(j, at, l):
+        return pltpu.make_async_copy(
+            cache_ref.at[l, j], out_ref.at[at, pl.ds(l * block_len, block_len)], sems.at[at, l]
+        )
+
     def send(j, carry):
         p, b = j // blocks, j % blocks
 
         @pl.when((b + 1) * block_len > window - len_ref[p, 0])
         def _():
-            peer = dest_ref[base + j] // per_dev
+            dest = dest_ref[base + j]
+            peer = dest // per_dev
             at = peer * capacity + count_ref[peer]
             count_ref[peer] = count_ref[peer] + 1
-            pltpu.make_async_copy(cache_ref.at[:, j], out_ref.at[at], sems.at[at]).start()
+            for l in range(layers):
+                block(j, at, l).start()
+            slot = jnp.full((rows - tail, lanes), dest - peer * per_dev, jnp.int32)
+            out_ref[at, pl.ds(tail, rows - tail)] = slot.astype(jnp.float32).astype(jnp.bfloat16)
 
         return carry
 
     lax.fori_loop(0, per_dev, send, 0)
 
     def done(j, carry):
-        pltpu.make_async_copy(cache_ref.at[:, 0], out_ref.at[j], sems.at[j]).wait()
+        for l in range(layers):
+            block(0, j, l).wait()
         return carry
 
     lax.fori_loop(0, total, done, 0)
 
 
-def place_kernel(src_ref, in_ref, out_ref, zero_ref, sems):
+def place_kernel(slot_ref, in_ref, out_ref, src_ref, zero_ref, held_ref, in_sem, sems):
+    total, _, _ = in_ref.shape
+    layers, slots, block_len, _ = out_ref.shape
+    load = pltpu.make_async_copy(in_ref, held_ref, in_sem)
+    load.start()
     zero_ref[...] = jnp.zeros_like(zero_ref)
-    slots = out_ref.shape[1]
+
+    def clear(j, carry):
+        src_ref[j] = -1
+        return carry
+
+    lax.fori_loop(0, slots, clear, 0)
+
+    def note(j, carry):
+        src_ref[slot_ref[j]] = j
+        return carry
+
+    lax.fori_loop(0, total, note, 0)
+
+    def fill(j, carry):
+        @pl.when(src_ref[j] < 0)
+        def _():
+            for l in range(layers):
+                pltpu.make_async_copy(zero_ref, out_ref.at[l, j], sems.at[l, j]).start()
+
+        return carry
+
+    lax.fori_loop(0, slots, fill, 0)
+    load.wait()
 
     def send(j, carry):
-        src = src_ref[j]
-
-        @pl.when(src >= 0)
-        def _():
-            pltpu.make_async_copy(in_ref.at[src], out_ref.at[:, j], sems.at[j]).start()
-
-        @pl.when(src < 0)
-        def _():
-            pltpu.make_async_copy(zero_ref, out_ref.at[:, j], sems.at[j]).start()
-
-        return carry
-
-    lax.fori_loop(0, slots, send, 0)
+        for l in range(layers):
+            held = held_ref.at[j, pl.ds(l * block_len, block_len)]
+            slot = slot_ref[j]
+            pltpu.make_async_copy(held, out_ref.at[l, slot], sems.at[l, slot]).start()
+        return carry
+
+    lax.fori_loop(0, total, send, 0)
 
     def done(j, carry):
-        pltpu.make_async_copy(zero_ref, out_ref.at[:, j], sems.at[j]).wait()
+        for l in range(layers):
+            pltpu.make_async_copy(zero_ref, out_ref.at[l, j], sems.at[l, j]).wait()
         return carry
 
     lax.fori_loop(0, slots, done, 0)
@@ -266,7 +313,6 @@
     prompts = lengths.shape[0]
     fresh_rows = tokens.shape[0] // prompts
     layers, _, blocks_win, block_len, lane_width = kv_cache.shape
-    window = blocks_win * block_len
     per_dev = prompts * blocks_win
     devices = lax.axis_size(("group", "dp"))
     capacity = per_dev // devices // 2
@@ -277,19 +323,20 @@
 
     smem = pl.BlockSpec(memory_space=pltpu.SMEM)
     hbm = pl.BlockSpec(memory_space=pltpu.HBM)
+    rows = layers * block_len + 16
     outgoing = pl.pallas_call(
         pick_kernel,
         in_specs=[smem, smem, smem, hbm],
-        out_specs=hbm,
-        out_shape=jax.ShapeDtypeStruct((total, layers, block_len, lane_width), jnp.bfloat16),
-        scratch_shapes=[pltpu.SMEM((devices,), jnp.int32), pltpu.SemaphoreType.DMA((total,))],
+        out_specs=pl.BlockSpec(memory_space=pltpu.VMEM),
+        out_shape=jax.ShapeDtypeStruct((total, rows, lane_width), jnp.bfloat16),
+        scratch_shapes=[
+            pltpu.SMEM((devices,), jnp.int32),
+            pltpu.SemaphoreType.DMA((total, layers)),
+        ],
+        compiler_params=pltpu.CompilerParams(vmem_limit_bytes=VMEM_LIMIT),
         cost_estimate=pl.CostEstimate(flops=0, bytes_accessed=10**7, transcendentals=0),
         name="pick",
     )(me.reshape(1), dest_flat, lengths, raw)
-    flat = jnp.zeros((8 * 128,), jnp.float32).at[: lengths.size].set(
-        lengths.reshape(-1).astype(jnp.float32)
-    )
-    tiles = lax.all_gather(flat.reshape(8, 128), ("group", "dp"), axis=0)
     norm_gain, outgoing = lax.optimization_barrier((norm_gain, outgoing))
     incoming = lax.all_to_all(outgoing, ("group", "dp"), split_axis=0, concat_axis=0, tiled=True)
 
@@ -317,32 +364,23 @@
         order.append((t - step + t_size) % t_size)
     mixed = mix(parts, jnp.stack(order), w_all)
 
-    lengths_every = tiles.reshape(devices, -1)[:, : lengths.size].reshape(devices * prompts, -1)
-    lengths_every = lengths_every.astype(jnp.int32)
-    dest_all = dest_slot.reshape(devices, per_dev)
-    recv_all = dest_all // per_dev
-    live_all = (
-        (jnp.arange(blocks_win)[None, :] + 1) * block_len > window - lengths_every[:, 0:1]
-    ).reshape(devices, per_dev)
-    same = recv_all[:, :, None] == recv_all[:, None, :]
-    earlier = jnp.arange(per_dev)[None, :] < jnp.arange(per_dev)[:, None]
-    rank = jnp.sum(same & earlier[None] & live_all[:, None, :], axis=2, dtype=jnp.int32)
-    where_from = jnp.arange(devices, dtype=jnp.int32)[:, None] * capacity + rank
-    slot = jnp.where((recv_all == me) & live_all, dest_all - me * per_dev, -1)
-    hit = slot.reshape(1, -1) == jnp.arange(per_dev, dtype=jnp.int32)[:, None]
-    source = jnp.max(jnp.where(hit, where_from.reshape(1, -1), -1), axis=1)
+    slots = incoming[:, layers * block_len, 0].astype(jnp.int32)
     decode_cache = pl.pallas_call(
         place_kernel,
         in_specs=[smem, hbm],
         out_specs=hbm,
         out_shape=jax.ShapeDtypeStruct((layers, per_dev, block_len, lane_width), jnp.bfloat16),
         scratch_shapes=[
-            pltpu.VMEM((layers, block_len, lane_width), jnp.bfloat16),
-            pltpu.SemaphoreType.DMA((per_dev,)),
-        ],
+            pltpu.SMEM((per_dev,), jnp.int32),
+            pltpu.VMEM((block_len, lane_width), jnp.bfloat16),
+            pltpu.VMEM((total, rows, lane_width), jnp.bfloat16),
+            pltpu.SemaphoreType.DMA,
+            pltpu.SemaphoreType.DMA((layers, per_dev)),
+        ],
+        compiler_params=pltpu.CompilerParams(vmem_limit_bytes=VMEM_LIMIT),
         cost_estimate=pl.CostEstimate(flops=0, bytes_accessed=10**7, transcendentals=0),
         name="place",
-    )(*lax.optimization_barrier((source, incoming, part))[:2])
+    )(slots, lax.optimization_barrier((incoming, part))[0])
     return (mixed, decode_cache)
 
 

time: 357 us -> 131 us (0.37)
  Pallas kernels: 298 us -> 59.1 us
  waiting for transfers between devices: 0.05 us -> 23.4 us
  blocking collectives: 14.6 us -> 0 us
  starting transfers between devices: 14.1 us -> 22.2 us
    pallas_call x1, Pallas kernels: 129 us -> 4.71 us  [per_device(): pl.pallas_call(pick_kernel, in_specs=[smem, smem, smem, hbm], out_specs=p...]
    pallas_call x1, Pallas kernels: 129 us -> 9.07 us  [per_device(): pl.pallas_call(place_kernel, in_specs=[smem, hbm], out_specs=hbm, out_sha...]
    all_gather x1, waiting for transfers between devices: 0.02 us -> 23.4 us  [per_device(): lax.all_gather(half, ('dp', 'tensor'), axis=0)]
    all_gather x1 -> x0, blocking collectives: 14.6 us -> none  [per_device(): tiles = lax.all_gather(flat.reshape(8, 128), ('group', 'dp'), axis=0)]
    ppermute x3, starting transfers between devices: 9.44 us -> 17.5 us  [per_device(): lax.ppermute(part, 'tensor', shift(step))]
    pallas_call x4, Pallas kernels: 26.3 us -> 32.2 us  [attend(): pl.pallas_call(attend_kernel, grid_spec=pltpu.PrefetchScalarGridSpec(num_...]
  transfers between devices with their start and end apart: 5 -> 5, of which waited for: 0 -> 1; matrix products, arithmetic and copies ran while one was open for 2% -> 3% of each run, Pallas kernels for 83% -> 41%
where the time goes in v2:
time: 131 us; the launch traced here: 129 us
  Pallas kernels  59.1 us (45%)
  waiting for transfers between devices  23.4 us (18%)
  starting transfers between devices  22.2 us (17%)
  between operations  14.3 us (11%)
  local copies, waits for them, and re-layouts  8.13 us (6%)
  other arithmetic  1.81 us (1%)
    pallas_call x4, Pallas kernels, attend(): pl.pallas_call(attend_kernel, grid_spec=pltpu.PrefetchScalarGridSpec(num_...  32.2 us
    all_gather x1, waiting for transfers between devices, per_device(): lax.all_gather(half, ('dp', 'tensor'), axis=0)  23.4 us
    ppermute x3, starting transfers between devices, per_device(): lax.ppermute(part, 'tensor', shift(step))  17.5 us
    pallas_call x1, Pallas kernels, per_device(): pl.pallas_call(place_kernel, in_specs=[smem, hbm], out_specs=hbm, out_sha...  9.07 us
    unnamed x14, local copies, waits for them, and re-layouts  6.74 us
    pallas_call x1, Pallas kernels, project(): pl.pallas_call(project_kernel, grid=(rows // fresh_rows,), in_specs=[pl.B...  6.71 us
    pallas_call x1, Pallas kernels, mix(): pl.pallas_call(mix_kernel, grid=(width // tile,), in_specs=[part] * len(p...  6.43 us
    pallas_call x1, Pallas kernels, per_device(): pl.pallas_call(pick_kernel, in_specs=[smem, smem, smem, hbm], out_specs=p...  4.71 us
  transfers between devices with their start and end apart: 5, of which 1 were waited for; matrix products, arithmetic and copies ran while one was open for 3% of the time, Pallas kernels for 41%

profile of v2, /device:TPU:6, one launch (start us, length us, event | category | flops | bytes accessed | tf_op | source)
XLA Modules:
  0.0 128.9 jit_solution(18240736422599628706)
XLA Ops:
  7.2 0.0 copy-start
  7.2 0.0 all-gather.3.cloned.1.call-start
  7.2 1.5 %copy-done = bf16[512,2048]{1,0:T(8,128)(2,1)S(1)} copy-done((bf16[512,2048]{1,0:T(8,128)(2,1)S(1)}, bf16[512,2048]{1,0:T(8,128)(2,1)}, u32[]{:S(2)}) %copy-start) | copy-done | bytes 2097176
  8.8 1.1 constant_dynamic-slice_fusion
  9.8 0.0 all-gather.3.cloned.1.call-update
  9.9 0.8 copy.11
  10.6 0.1 reshape.35.dest_ref
  10.7 0.8 copy.12.len_ref
  11.5 4.7 %pick.1 = bf16[32,528,128]{2,1,0:T(8,128)(2,1)S(1)} custom-call(s32[1]{0:T(128)} %bitcast.1.me_ref, s32[512]{0:T(512)S(1)} %reshape.35.dest_ref, s32[4,2]{1,0:T(4,128)S(1)} %copy.12.len_ref, bf16[4,64,128,128]{3,2,1,0:T(8,128)(2,1)} %bitcast.8), custom_call_target="tpu_custom_call" | custom-call | bytes 10000000 | tf_op jit(solution)/shard_map/pick/pallas_call | solution.py:327
  16.2 0.0 copy-start.1
  16.2 2.0 %copy-done.1 = bf16[32,528,128]{2,1,0:T(8,128)(2,1)} copy-done((bf16[32,528,128]{2,1,0:T(8,128)(2,1)}, bf16[32,528,128]{2,1,0:T(8,128)(2,1)S(1)}, u32[]{:S(2)}) %copy-start.1) | copy-done | bytes 4325400
  18.3 0.0 copy-start.5
  18.3 0.0 copy-start.4
  18.3 0.0 copy-start.3
  18.3 4.7 %all-to-all-start = ((bf16[32,528,128]{2,1,0:T(8,128)(2,1)}), bf16[32,528,128]{2,1,0:T(8,128)(2,1)}, u32[]{:S(2)}, u32[]{:S(2)}) async-start(bf16[32,528,128]{2,1,0:T(8,128)(2,1)} %copy-done.1), calls=%async_computation | async-start | bytes 8650752 | tf_op jit(solution)/shard_map/all_to_all | solution.py:341
  23.0 0.0 copy-done.5
  23.0 0.0 copy-done.4
  23.0 0.2 fusion.4
  23.3 0.1 pad_add_fusion.info_ref
  23.3 0.0 copy-done.3
  23.3 0.0 copy-start.2
  23.3 1.6 %copy-done.2 = bf16[2048,512]{1,0:T(8,128)(2,1)S(1)} copy-done((bf16[2048,512]{1,0:T(8,128)(2,1)S(1)}, bf16[2048,512]{1,0:T(8,128)(2,1)}, u32[]{:S(2)}) %copy-start.2) | copy-done | bytes 2097176
  24.9 6.7 %project.1 = (bf16[8,1024,128]{2,1,0:T(8,128)(2,1)S(1)}, bf16[1024,128]{1,0:T(8,128)(2,1)S(1)}) custom-call(bf16[1024,2048]{1,0:T(8,128)(2,1)} %tok_ref.1, bf16[1,2048]{1,0:T(2,128)(2,1)S(1)} %reshape.37.gain_ref, bf16[2048,512]{1,0:T(8,128)(2,1)S(1)} %copy-done.2, bf16[2048,128]{1,0:T(8,128)(2,1)S(1)} %copy-done.3), custom_call_target="tpu_custom_call" | custom-call | flops 2684354560 | bytes 10000000 | tf_op jit(solution)/shard_map/project/pallas_call | solution.py:33
  31.7 3.1 %attend.4 = bf16[256,512]{1,0:T(8,128)(2,1)S(1)} custom-call(s32[3]{0:T(128)S(1)} %pad_add_fusion.info_ref, bf16[8,1024,128]{2,1,0:T(8,128)(2,1)S(1)} %get-tuple-element.11.q_ref, bf16[1024,128]{1,0:T(8,128)(2,1)S(1)} %get-tuple-element.12.kv_ref, bf16[4,4,16,128,128]{4,3,2,1,0:T(8,128)(2,1)} %cache_ref.7), custom_call_target="tpu_custom_call" | custom-call | flops 1000000000 | bytes 1000000 | tf_op jit(solution)/shard_map/attend/pallas_call | solution.py:155
  34.8 7.8 %collective-permute-start = (bf16[256,512]{1,0:T(8,128)(2,1)S(1)}, bf16[256,512]{1,0:T(8,128)(2,1)S(1)}, u32[]{:S(2)}, u32[]{:S(2)}) collective-permute-start(bf16[256,512]{1,0:T(8,128)(2,1)S(1)} %attend.4), channel_id=1, source_target_pairs={{0,1},{1,2},{2,3},{3,0},{4,5},{5,6},{6,7},{7,4},{8,9},{9,10},{10,1... | collective-permute-start | bytes 786440 | tf_op jit(solution)/shard_map/ppermute | solution.py:363
  42.5 0.1 pad_add_fusion.1
  42.6 8.9 %attend.5 = bf16[256,512]{1,0:T(8,128)(2,1)S(1)} custom-call(s32[3]{0:T(128)S(1)} %get-tuple-element.13.info_ref, bf16[8,1024,128]{2,1,0:T(8,128)(2,1)S(1)} %get-tuple-element.11.q_ref, bf16[1024,128]{1,0:T(8,128)(2,1)S(1)} %get-tuple-element.12.kv_ref, bf16[4,4,16,128,128]{4,3,2,1,0:T(8,128)(2,1)} %cache_ref.7), custom_call_target="tpu_custom_call" | custom-call | flops 1000000000 | bytes 1000000 | tf_op jit(solution)/shard_map/attend/pallas_call | solution.py:155
  51.5 9.7 %collective-permute-start.1 = (bf16[256,512]{1,0:T(8,128)(2,1)S(1)}, bf16[256,512]{1,0:T(8,128)(2,1)}, u32[]{:S(2)}, u32[]{:S(2)}) collective-permute-start(bf16[256,512]{1,0:T(8,128)(2,1)S(1)} %attend.5), channel_id=1, source_target_pairs={{0,2},{1,3},{2,0},{3,1},{4,6},{5,7},{6,4},{7,5},{8,10},{9,11},{10,... | collective-permute-start | bytes 786440 | tf_op jit(solution)/shard_map/ppermute | solution.py:363
  61.2 7.7 %attend.6 = bf16[256,512]{1,0:T(8,128)(2,1)S(1)} custom-call(s32[3]{0:T(128)S(1)} %get-tuple-element.14.info_ref, bf16[8,1024,128]{2,1,0:T(8,128)(2,1)S(1)} %get-tuple-element.11.q_ref, bf16[1024,128]{1,0:T(8,128)(2,1)S(1)} %get-tuple-element.12.kv_ref, bf16[4,4,16,128,128]{4,3,2,1,0:T(8,128)(2,1)} %cache_ref.7), custom_call_target="tpu_custom_call" | custom-call | flops 1000000000 | bytes 1000000 | tf_op jit(solution)/shard_map/attend/pallas_call | solution.py:155
  68.9 0.1 collective-permute-start.2
  69.0 0.1 pad_add_fusion.3.info_ref
  69.1 12.5 %attend.7.d_ref = bf16[256,512]{1,0:T(8,128)(2,1)S(1)} custom-call(s32[3]{0:T(128)S(1)} %pad_add_fusion.3.info_ref, bf16[8,1024,128]{2,1,0:T(8,128)(2,1)S(1)} %get-tuple-element.11.q_ref, bf16[1024,128]{1,0:T(8,128)(2,1)S(1)} %get-tuple-element.12.kv_ref, bf16[4,4,16,128,128]{4,3,2,1,0:T(8,128)(2,1)} %cache_ref.7), custom_call_target="tpu_custom_call" | custom-call | flops 1000000000 | bytes 1000000 | tf_op jit(solution)/shard_map/attend/pallas_call | solution.py:155
  81.6 0.1 pad_add_fusion.4.order_ref
  81.6 0.0 all-to-all-done.in_ref
  81.6 1.5 %fusion.slot_ref = s32[32]{0:T(128)S(1)} fusion(bf16[32,528,128]{2,1,0:T(8,128)(2,1)} %all-to-all-done.in_ref), kind=kLoop, calls=%fused_computation.1 | loop fusion | flops 32 | bytes 192 | tf_op jit(solution)/shard_map/convert_element_type | solution.py:367
  83.1 9.1 %place.1 = bf16[4,64,128,128]{3,2,1,0:T(8,128)(2,1)} custom-call(s32[32]{0:T(128)S(1)} %fusion.slot_ref, bf16[32,528,128]{2,1,0:T(8,128)(2,1)} %all-to-all-done.in_ref), custom_call_target="tpu_custom_call" | custom-call | bytes 10000000 | tf_op jit(solution)/shard_map/place/pallas_call | solution.py:368
  92.2 0.0 collective-permute-done.a_ref
  92.2 0.0 collective-permute-done.1.b_ref
  92.2 0.0 collective-permute-done.2.c_ref
  92.3 23.4 %all-gather.3.cloned.1.call-done = bf16[2048,2048]{1,0:T(8,128)(2,1)} async-done(((bf16[256,2048]{1,0:T(8,128)(2,1)}), bf16[2048,2048]{1,0:T(8,128)(2,1)}) %all-gather.3.cloned.1.call-update) | async-done | bytes 8388624 | tf_op jit(solution)/shard_map/all_gather | solution.py:346
  115.6 6.4 %mix.1 = bf16[256,2048]{1,0:T(8,128)(2,1)} custom-call(bf16[256,512]{1,0:T(8,128)(2,1)S(1)} %collective-permute-done.a_ref, bf16[256,512]{1,0:T(8,128)(2,1)} %collective-permute-done.1.b_ref, bf16[256,512]{1,0:T(8,128)(2,1)} %collective-permute-done.2.c_ref, bf16[256,512]{1,0:T(8,128)(2,1)S(1)} %attend.7.d_ref, s32[4]{0:T(128)S(1)} %pad_add_fusion.4.order_ref, ...), custom_call_target="tpu_custom_call" | custom-call | flops 2147483648 | bytes 10000000 | tf_op jit(solution)/shard_map/mix/pallas_call | solution.py:294
  (1 shorter events, 0.0 us)
Async XLA Ops:
  7.2 1.6 %copy-start = (bf16[512,2048]{1,0:T(8,128)(2,1)S(1)}, bf16[512,2048]{1,0:T(8,128)(2,1)}, u32[]{:S(2)}) copy-start(bf16[512,2048]{1,0:T(8,128)(2,1)} %param.12) | copy-start | bytes 6291460
  7.2 108.5 %all-gather.3.cloned.1.call-start = ((), (), s32[]{:S(2)}) async-start(), calls=%async_computation.1 | async-start | bytes 9437184 | tf_op jit(solution)/shard_map/all_gather | solution.py:346
  16.2 2.1 %copy-start.1 = (bf16[32,528,128]{2,1,0:T(8,128)(2,1)}, bf16[32,528,128]{2,1,0:T(8,128)(2,1)S(1)}, u32[]{:S(2)}) copy-start(bf16[32,528,128]{2,1,0:T(8,128)(2,1)S(1)} %pick.1) | copy-start | bytes 12976132
  18.3 4.7 %copy-start.5 = (bf16[2048]{0:T(1024)(128)(2,1)S(1)}, bf16[2048]{0:T(1024)(128)(2,1)}, u32[]{:S(2)}) copy-start(bf16[2048]{0:T(1024)(128)(2,1)} %param.9) | copy-start | bytes 12292
  18.3 4.8 %copy-start.4 = (s32[4,2]{0,1:T(2,128)S(1)}, s32[4,2]{0,1:T(2,128)}, u32[]{:S(2)}) copy-start(s32[4,2]{0,1:T(2,128)} %param.14) | copy-start | bytes 100
  18.3 5.1 %copy-start.3 = (bf16[2048,128]{1,0:T(8,128)(2,1)S(1)}, bf16[2048,128]{1,0:T(8,128)(2,1)}, u32[]{:S(2)}) copy-start(bf16[2048,128]{1,0:T(8,128)(2,1)} %wkv_ref.1) | copy-start | bytes 1572868
  18.3 63.4 %all-to-all-start = ((bf16[32,528,128]{2,1,0:T(8,128)(2,1)}), bf16[32,528,128]{2,1,0:T(8,128)(2,1)}, u32[]{:S(2)}, u32[]{:S(2)}) async-start(bf16[32,528,128]{2,1,0:T(8,128)(2,1)} %copy-done.1), calls=%async_computation | async-start | bytes 8650752 | tf_op jit(solution)/shard_map/all_to_all | solution.py:341
  23.3 1.6 %copy-start.2 = (bf16[2048,512]{1,0:T(8,128)(2,1)S(1)}, bf16[2048,512]{1,0:T(8,128)(2,1)}, u32[]{:S(2)}) copy-start(bf16[2048,512]{1,0:T(8,128)(2,1)} %wq_ref.1) | copy-start | bytes 6291460
  34.8 57.5 %collective-permute-start = (bf16[256,512]{1,0:T(8,128)(2,1)S(1)}, bf16[256,512]{1,0:T(8,128)(2,1)S(1)}, u32[]{:S(2)}, u32[]{:S(2)}) collective-permute-start(bf16[256,512]{1,0:T(8,128)(2,1)S(1)} %attend.4), channel_id=1, source_target_pairs={{0,1},{1,2},{2,3},{3,0},{4,5},{5,6},{6,7},{7,4},{8,9},{9,10},{10,1... | collective-permute-start | bytes 786440 | tf_op jit(solution)/shard_map/ppermute | solution.py:363
  51.5 40.7 %collective-permute-start.1 = (bf16[256,512]{1,0:T(8,128)(2,1)S(1)}, bf16[256,512]{1,0:T(8,128)(2,1)}, u32[]{:S(2)}, u32[]{:S(2)}) collective-permute-start(bf16[256,512]{1,0:T(8,128)(2,1)S(1)} %attend.5), channel_id=1, source_target_pairs={{0,2},{1,3},{2,0},{3,1},{4,6},{5,7},{6,4},{7,5},{8,10},{9,11},{10,... | collective-permute-start | bytes 786440 | tf_op jit(solution)/shard_map/ppermute | solution.py:363
  68.9 23.3 %collective-permute-start.2 = (bf16[256,512]{1,0:T(8,128)(2,1)S(1)}, bf16[256,512]{1,0:T(8,128)(2,1)}, u32[]{:S(2)}, u32[]{:S(2)}) collective-permute-start(bf16[256,512]{1,0:T(8,128)(2,1)S(1)} %attend.6), channel_id=1, source_target_pairs={{0,3},{1,0},{2,1},{3,2},{4,7},{5,4},{6,5},{7,6},{8,11},{9,8},{10,9... | collective-permute-start | bytes 786440 | tf_op jit(solution)/shard_map/ppermute | solution.py:363
Sparse Core Ops, SparseCore 0:
  10.2 105.4 all-gather.2

commit v3 on v2

--- a/solution.py
+++ b/solution.py
@@ -1,3 +1,5 @@
+import functools
+
 import jax
 import jax.numpy as jnp
 from jax import lax
@@ -271,34 +273,59 @@
     lax.fori_loop(0, slots, done, 0)
 
 
-def mix_kernel(a_ref, b_ref, c_ref, d_ref, order_ref, w_ref, out_ref):
+def mix_kernel(n_parts, n_cut, *refs):
+    parts, refs = refs[:n_parts], refs[n_parts:]
+    order_ref, w_ref, own_ref, refs = refs[0], refs[1], refs[2], refs[3:]
+    pieces, out_ref = refs[:-1], refs[-1]
     halves, shards, depth, _ = w_ref.shape
-    total = None
-    for ref, k in ((a_ref, 0), (b_ref, 1), (c_ref, 2), (d_ref, 3)):
-        t = order_ref[k]
-        for half in range(halves):
-            term = jnp.dot(
-                ref[:, half * depth : (half + 1) * depth],
-                w_ref[half, t],
-                preferred_element_type=jnp.float32,
-            )
-            total = term if total is None else total + term
-    out_ref[...] = total.astype(jnp.bfloat16)
-
-
-def mix(parts, order, w_all):
+
+    def dot(a, b):
+        return jnp.dot(a, b, preferred_element_type=jnp.float32)
+
+    gathered = pl.program_id(0) < pl.num_programs(0) // 2
+
+    @pl.when(gathered)
+    def _():
+        total = jnp.zeros(out_ref.shape, jnp.float32)
+        for k, part in enumerate(parts):
+            for half in range(halves):
+                cut = part[:, half * depth : (half + 1) * depth]
+                total = total + dot(cut, w_ref[half, order_ref[k]])
+        out_ref[...] = total.astype(jnp.bfloat16)
+
+    @pl.when(jnp.logical_not(gathered))
+    def _():
+        total = dot(parts[-1][...], own_ref[...])
+        for k in range(n_parts - 1):
+            for c in range(n_cut):
+                piece = pieces[k * n_cut + c]
+                rows = piece.shape[0]
+                at = pl.multiple_of(order_ref[n_parts + c] * rows, rows)
+                total = total + dot(parts[k][:, pl.ds(at, rows)], piece[...])
+        out_ref[...] = total.astype(jnp.bfloat16)
+
+
+def mix(parts, order, w_all, w_out, pieces, n_cut):
     rows, depth = parts[0].shape
-    halves, shards, half_depth, width = w_all.shape
+    halves, shards, half_depth, _ = w_all.shape
+    width = w_out.shape[1]
     tile = 512
+    tiles = width // tile
+    first = tiles // 2
     part = pl.BlockSpec((rows, depth), lambda i: (0, 0))
+    piece = pl.BlockSpec((pieces[0].shape[0], tile), lambda i: (0, jnp.maximum(i - first, 0)))
     return pl.pallas_call(
-        mix_kernel,
-        grid=(width // tile,),
+        functools.partial(mix_kernel, len(parts), n_cut),
+        grid=(tiles,),
         in_specs=[part] * len(parts)
         + [
             pl.BlockSpec(memory_space=pltpu.SMEM),
-            pl.BlockSpec((halves, shards, half_depth, tile), lambda i: (0, 0, 0, i)),
-        ],
+            pl.BlockSpec(
+                (halves, shards, half_depth, tile), lambda i: (0, 0, 0, jnp.minimum(i, first - 1))
+            ),
+            pl.BlockSpec((depth, tile), lambda i: (0, jnp.maximum(i, first))),
+        ]
+        + [piece] * len(pieces),
         out_specs=pl.BlockSpec((rows, tile), lambda i: (0, i)),
         out_shape=jax.ShapeDtypeStruct((rows, width), jnp.bfloat16),
         compiler_params=pltpu.CompilerParams(vmem_limit_bytes=VMEM_LIMIT),
@@ -306,7 +333,7 @@
             flops=2 * rows * depth * 4 * width, bytes_accessed=10**7, transcendentals=0
         ),
         name="mix",
-    )(*parts, order, w_all)
+    )(*parts, order, w_all, w_out, *pieces)
 
 
 def per_device(tokens, norm_gain, w_query, w_keyval, w_out, kv_cache, lengths, dest_slot):
@@ -340,29 +367,42 @@
     norm_gain, outgoing = lax.optimization_barrier((norm_gain, outgoing))
     incoming = lax.all_to_all(outgoing, ("group", "dp"), split_axis=0, concat_axis=0, tiled=True)
 
+    t_size = lax.axis_size("tensor")
+
+    def shift(by):
+        return [(i, (i + by) % t_size) for i in range(t_size)]
+
     cores = lax.axis_size("dp")
+    core = lax.axis_index("dp").astype(jnp.int32)
     depth = w_out.shape[0] // cores
-    half = lax.dynamic_slice_in_dim(w_out, lax.axis_index("dp") * depth, depth, 0)
+    split = w_out.shape[1] // 2
+    half = lax.dynamic_slice(w_out, (core * depth, 0), (depth, split))
     w_all = lax.all_gather(half, ("dp", "tensor"), axis=0).reshape(cores, -1, *half.shape)
+    if cores == 2:
+        mine = lax.dynamic_slice(w_out, (core * depth, split), (depth, split))
+        places = [core, 1 - core]
+    else:
+        mine = w_out[:, split:]
+        places = [jnp.zeros((), jnp.int32)]
+    sent = [lax.ppermute(mine, "tensor", shift(step)) for step in range(1, t_size)]
 
     query, keyval = project(tokens, norm_gain, w_query, w_keyval, fresh_rows)
-    t_size = lax.axis_size("tensor")
     t = lax.axis_index("tensor").astype(jnp.int32)
     parts, order = [], []
-
-    def shift(by):
-        return [(i, (i + by) % t_size) for i in range(t_size)]
-
     for step in range(1, t_size + 1):
         p = (t + step) % t_size
         own = lax.dynamic_index_in_dim(lengths, p, 0, keepdims=False)
         info = jnp.concatenate([p.reshape(1), own])
         if step > 1:
             info = lax.optimization_barrier((info, part))[0]
+        if step == t_size and cores == 2:
+            info, *sent = lax.optimization_barrier((info, *sent))
+            swapped = [lax.ppermute(piece, "dp", [(0, 1), (1, 0)]) for piece in sent]
+            sent = [piece for pair in zip(sent, swapped) for piece in pair]
         part = attend(info, query, keyval, kv_cache)
         parts.append(lax.ppermute(part, "tensor", shift(step)) if step < t_size else part)
         order.append((t - step + t_size) % t_size)
-    mixed = mix(parts, jnp.stack(order), w_all)
+    mixed = mix(parts, jnp.stack(order + places), w_all, w_out, sent, len(places))
 
     slots = incoming[:, layers * block_len, 0].astype(jnp.int32)
     decode_cache = pl.pallas_call(

time: 131 us -> 148 us (1.13)
  starting transfers between devices: 22.2 us -> 44.1 us
  waiting for transfers between devices: 23.4 us -> 19.6 us
    all_gather x1, waiting for transfers between devices: 23.4 us -> 0.02 us  [per_device(): lax.all_gather(half, ('dp', 'tensor'), axis=0)]
    ppermute x0 -> x6, waiting for transfers between devices: none -> 19.6 us  [the longest x3 19.6 us: per_device(): lax.ppermute(mine, 'tensor', shift(step))]
    ppermute x3, starting transfers between devices: 17.5 us -> 32.5 us  [per_device(): lax.ppermute(part, 'tensor', shift(step))]
    ppermute x0 -> x6, starting transfers between devices: none -> 6.76 us  [the longest x3 6.25 us: per_device(): lax.ppermute(mine, 'tensor', shift(step))]
    unnamed x14 -> x12, local copies, waits for them, and re-layouts: 6.74 us -> 6.23 us
  transfers between devices with their start and end apart: 5 -> 11, of which waited for: 1 -> 1; matrix products, arithmetic and copies ran while one was open for 3% -> 2% of each run, Pallas kernels for 41% -> 35%
where the time goes in v3:
time: 148 us; the launch traced here: 147 us
  Pallas kernels  58.8 us (40%)
  starting transfers between devices  44.1 us (30%)
  waiting for transfers between devices  19.6 us (13%)
  between operations  14.2 us (10%)
  local copies, waits for them, and re-layouts  8.88 us (6%)
  other arithmetic  1.73 us (1%)
    ppermute x3, starting transfers between devices, per_device(): lax.ppermute(part, 'tensor', shift(step))  32.5 us
    pallas_call x4, Pallas kernels, attend(): pl.pallas_call(attend_kernel, grid_spec=pltpu.PrefetchScalarGridSpec(num_...  32.4 us
    ppermute x3, waiting for transfers between devices, per_device(): lax.ppermute(mine, 'tensor', shift(step))  19.6 us
    pallas_call x1, Pallas kernels, per_device(): pl.pallas_call(place_kernel, in_specs=[smem, hbm], out_specs=hbm, out_sha...  8.63 us
    pallas_call x1, Pallas kernels, mix(): pl.pallas_call(functools.partial(mix_kernel, len(parts), n_cut), grid=(ti...  6.78 us
    pallas_call x1, Pallas kernels, project(): pl.pallas_call(project_kernel, grid=(rows // fresh_rows,), in_specs=[pl.B...  6.58 us
    ppermute x3, starting transfers between devices, per_device(): lax.ppermute(mine, 'tensor', shift(step))  6.25 us
    unnamed x12, local copies, waits for them, and re-layouts  6.23 us
  transfers between devices with their start and end apart: 11, of which 1 were waited for; matrix products, arithmetic and copies ran while one was open for 2% of the time, Pallas kernels for 35%

profile of v3, /device:TPU:6, one launch (start us, length us, event | category | flops | bytes accessed | tf_op | source)
XLA Modules:
  0.0 147.3 jit_solution(8416721498912377431)
XLA Ops:
  7.2 0.0 all-gather.3.cloned.1.call-start
  7.2 2.3 %constant_dynamic-slice_fusion = (bf16[256,1024]{1,0:T(8,128)(2,1)}, bf16[256,1024]{1,0:T(8,128)(2,1)}) fusion(bf16[512,2048]{1,0:T(8,128)(2,1)} %refs_6_.1, s32[]{:T(128)S(6)} %select_n.54), kind=kLoop, calls=%fused_computation.2 | loop fusion | bytes 2097156 | tf_op jit(solution)/shard_map/dynamic_slice | solution.py:379
  9.5 0.0 all-gather.3.cloned.1.call-update
  9.5 0.8 copy.11
  10.3 0.1 reshape.35.dest_ref
  10.4 0.8 copy.12.len_ref
  11.1 4.4 %pick.1 = bf16[32,528,128]{2,1,0:T(8,128)(2,1)S(1)} custom-call(s32[1]{0:T(128)} %bitcast.1.me_ref, s32[512]{0:T(512)S(1)} %reshape.35.dest_ref, s32[4,2]{1,0:T(4,128)S(1)} %copy.12.len_ref, bf16[4,64,128,128]{3,2,1,0:T(8,128)(2,1)} %bitcast.10), custom_call_target="tpu_custom_call" | custom-call | bytes 10000000 | tf_op jit(solution)/shard_map/pick/pallas_call | solution.py:354
  15.6 0.0 copy-start
  15.6 2.0 %copy-done = bf16[32,528,128]{2,1,0:T(8,128)(2,1)} copy-done((bf16[32,528,128]{2,1,0:T(8,128)(2,1)}, bf16[32,528,128]{2,1,0:T(8,128)(2,1)S(1)}, u32[]{:S(2)}) %copy-start) | copy-done | bytes 4325400
  17.6 4.8 %all-to-all-start = ((bf16[32,528,128]{2,1,0:T(8,128)(2,1)}), bf16[32,528,128]{2,1,0:T(8,128)(2,1)}, u32[]{:S(2)}, u32[]{:S(2)}) async-start(bf16[32,528,128]{2,1,0:T(8,128)(2,1)} %copy-done), calls=%async_computation | async-start | bytes 8650752 | tf_op jit(solution)/shard_map/all_to_all | solution.py:368
  22.4 2.3 %collective-permute-start.3 = (bf16[256,1024]{1,0:T(8,128)(2,1)}, bf16[256,1024]{1,0:T(8,128)(2,1)S(1)}, u32[]{:S(2)}, u32[]{:S(2)}) collective-permute-start(bf16[256,1024]{1,0:T(8,128)(2,1)} %get-tuple-element.31), channel_id=1, source_target_pairs={{0,1},{1,2},{2,3},{3,0},{4,5},{5,6},{6,7},{7,4},{8,9},{9,10},{10,1... | collective-permute-start | bytes 1572872 | tf_op jit(solution)/shard_map/ppermute | solution.py:387
  24.8 2.6 %collective-permute-start.4 = (bf16[256,1024]{1,0:T(8,128)(2,1)}, bf16[256,1024]{1,0:T(8,128)(2,1)}, u32[]{:S(2)}, u32[]{:S(2)}) collective-permute-start(bf16[256,1024]{1,0:T(8,128)(2,1)} %get-tuple-element.31), channel_id=1, source_target_pairs={{0,2},{1,3},{2,0},{3,1},{4,6},{5,7},{6,4},{7,5},{8,10},{9,11},{10,... | collective-permute-start | bytes 1572872 | tf_op jit(solution)/shard_map/ppermute | solution.py:387
  27.3 1.4 collective-permute-start.5
  28.7 0.0 copy-done.4
  28.7 0.0 copy-done.3
  28.7 0.2 fusion.4
  28.9 0.0 copy-start.1
  29.0 1.6 %copy-done.1 = bf16[2048,512]{1,0:T(8,128)(2,1)S(1)} copy-done((bf16[2048,512]{1,0:T(8,128)(2,1)S(1)}, bf16[2048,512]{1,0:T(8,128)(2,1)}, u32[]{:S(2)}) %copy-start.1) | copy-done | bytes 2097176
  30.5 1.0 copy-done.2
  31.6 6.6 %project.1 = (bf16[8,1024,128]{2,1,0:T(8,128)(2,1)S(1)}, bf16[1024,128]{1,0:T(8,128)(2,1)S(1)}) custom-call(bf16[1024,2048]{1,0:T(8,128)(2,1)} %tok_ref.1, bf16[1,2048]{1,0:T(2,128)(2,1)S(1)} %reshape.37.gain_ref, bf16[2048,512]{1,0:T(8,128)(2,1)S(1)} %copy-done.1, bf16[2048,128]{1,0:T(8,128)(2,1)S(1)} %copy-done.2), custom_call_target="tpu_custom_call" | custom-call | flops 2684354560 | bytes 10000000 | tf_op jit(solution)/shard_map/project/pallas_call | solution.py:35
  38.2 0.1 pad_add_fusion.info_ref
  38.2 3.1 %attend.4 = bf16[256,512]{1,0:T(8,128)(2,1)S(1)} custom-call(s32[3]{0:T(128)S(1)} %pad_add_fusion.info_ref, bf16[8,1024,128]{2,1,0:T(8,128)(2,1)S(1)} %get-tuple-element.15.q_ref, bf16[1024,128]{1,0:T(8,128)(2,1)S(1)} %get-tuple-element.16.kv_ref, bf16[4,4,16,128,128]{4,3,2,1,0:T(8,128)(2,1)} %cache_ref.7), custom_call_target="tpu_custom_call" | custom-call | flops 1000000000 | bytes 1000000 | tf_op jit(solution)/shard_map/attend/pallas_call | solution.py:157
  41.3 10.0 %collective-permute-start = (bf16[256,512]{1,0:T(8,128)(2,1)S(1)}, bf16[256,512]{1,0:T(8,128)(2,1)S(1)}, u32[]{:S(2)}, u32[]{:S(2)}) collective-permute-start(bf16[256,512]{1,0:T(8,128)(2,1)S(1)} %attend.4), channel_id=1, source_target_pairs={{0,1},{1,2},{2,3},{3,0},{4,5},{5,6},{6,7},{7,4},{8,9},{9,10},{10,1... | collective-permute-start | bytes 786440 | tf_op jit(solution)/shard_map/ppermute | solution.py:403
  51.3 0.1 pad_add_fusion.1
  51.4 13.0 %attend.5 = bf16[256,512]{1,0:T(8,128)(2,1)} custom-call(s32[3]{0:T(128)S(1)} %get-tuple-element.17.info_ref, bf16[8,1024,128]{2,1,0:T(8,128)(2,1)S(1)} %get-tuple-element.15.q_ref, bf16[1024,128]{1,0:T(8,128)(2,1)S(1)} %get-tuple-element.16.kv_ref, bf16[4,4,16,128,128]{4,3,2,1,0:T(8,128)(2,1)} %cache_ref.7), custom_call_target="tpu_custom_call" | custom-call | flops 1000000000 | bytes 1000000 | tf_op jit(solution)/shard_map/attend/pallas_call | solution.py:157
  64.4 3.8 %attend.6 = bf16[256,512]{1,0:T(8,128)(2,1)} custom-call(s32[3]{0:T(128)S(1)} %get-tuple-element.18.info_ref, bf16[8,1024,128]{2,1,0:T(8,128)(2,1)S(1)} %get-tuple-element.15.q_ref, bf16[1024,128]{1,0:T(8,128)(2,1)S(1)} %get-tuple-element.16.kv_ref, bf16[4,4,16,128,128]{4,3,2,1,0:T(8,128)(2,1)} %cache_ref.7), custom_call_target="tpu_custom_call" | custom-call | flops 1000000000 | bytes 1000000 | tf_op jit(solution)/shard_map/attend/pallas_call | solution.py:157
  68.2 0.1 pad_add_fusion.3.info_ref
  68.3 0.0 collective-permute-done.3.refs_7_
  68.3 19.6 %collective-permute-done.4.refs_9_ = bf16[256,1024]{1,0:T(8,128)(2,1)} collective-permute-done((bf16[256,1024]{1,0:T(8,128)(2,1)}, bf16[256,1024]{1,0:T(8,128)(2,1)}, u32[]{:S(2)}, u32[]{:S(2)}) %collective-permute-start.4) | collective-permute-done | bytes 524320 | tf_op jit(solution)/shard_map/ppermute | solution.py:387
  87.8 0.0 collective-permute-done.5.refs_11_
  87.8 0.0 collective-permute-start.6
  87.8 0.5 collective-permute-start.7
  88.3 0.0 collective-permute-start.8
  88.3 19.1 %collective-permute-start.1 = (bf16[256,512]{1,0:T(8,128)(2,1)}, bf16[256,512]{1,0:T(8,128)(2,1)}, u32[]{:S(2)}, u32[]{:S(2)}) collective-permute-start(bf16[256,512]{1,0:T(8,128)(2,1)} %attend.5), channel_id=1, source_target_pairs={{0,2},{1,3},{2,0},{3,1},{4,6},{5,7},{6,4},{7,5},{8,10},{9,11},{10,... | collective-permute-start | bytes 786440 | tf_op jit(solution)/shard_map/ppermute | solution.py:403
  107.5 0.0 collective-permute-done.refs_0_
  107.5 3.4 %collective-permute-start.2 = (bf16[256,512]{1,0:T(8,128)(2,1)}, bf16[256,512]{1,0:T(8,128)(2,1)}, u32[]{:S(2)}, u32[]{:S(2)}) collective-permute-start(bf16[256,512]{1,0:T(8,128)(2,1)} %attend.6), channel_id=1, source_target_pairs={{0,3},{1,0},{2,1},{3,2},{4,7},{5,4},{6,5},{7,6},{8,11},{9,8},{10,9... | collective-permute-start | bytes 786440 | tf_op jit(solution)/shard_map/ppermute | solution.py:403
  110.9 0.1 stack.18.refs_4_
  110.9 12.5 %attend.7.refs_3_ = bf16[256,512]{1,0:T(8,128)(2,1)S(1)} custom-call(s32[3]{0:T(128)S(1)} %pad_add_fusion.3.info_ref, bf16[8,1024,128]{2,1,0:T(8,128)(2,1)S(1)} %get-tuple-element.15.q_ref, bf16[1024,128]{1,0:T(8,128)(2,1)S(1)} %get-tuple-element.16.kv_ref, bf16[4,4,16,128,128]{4,3,2,1,0:T(8,128)(2,1)} %cache_ref.7), custom_call_target="tpu_custom_call" | custom-call | flops 1000000000 | bytes 1000000 | tf_op jit(solution)/shard_map/attend/pallas_call | solution.py:157
  123.4 0.0 all-to-all-done.in_ref
  123.5 1.5 %fusion.slot_ref = s32[32]{0:T(128)S(1)} fusion(bf16[32,528,128]{2,1,0:T(8,128)(2,1)} %all-to-all-done.in_ref), kind=kLoop, calls=%fused_computation.1 | loop fusion | flops 32 | bytes 192 | tf_op jit(solution)/shard_map/convert_element_type | solution.py:407
  125.0 8.6 %place.1 = bf16[4,64,128,128]{3,2,1,0:T(8,128)(2,1)} custom-call(s32[32]{0:T(128)S(1)} %fusion.slot_ref, bf16[32,528,128]{2,1,0:T(8,128)(2,1)} %all-to-all-done.in_ref), custom_call_target="tpu_custom_call" | custom-call | bytes 10000000 | tf_op jit(solution)/shard_map/place/pallas_call | solution.py:408
  133.6 0.0 collective-permute-done.1.refs_1_
  133.6 0.0 collective-permute-done.2.refs_2_
  133.6 0.0 collective-permute-done.6.refs_8_
  133.6 0.0 collective-permute-done.7.refs_10_
  133.6 0.0 collective-permute-done.8.refs_12_
  133.6 0.0 all-gather.3.cloned.1.call-done
  133.7 6.8 %mix.1 = bf16[256,2048]{1,0:T(8,128)(2,1)} custom-call(bf16[256,512]{1,0:T(8,128)(2,1)S(1)} %collective-permute-done.refs_0_, bf16[256,512]{1,0:T(8,128)(2,1)} %collective-permute-done.1.refs_1_, bf16[256,512]{1,0:T(8,128)(2,1)} %collective-permute-done.2.refs_2_, bf16[256,512]{1,0:T(8,128)(2,1)S(1)} %attend.7.refs_3_, s32[6]{0:T(128)S(1)} %stack.18.refs_4_, ...), custom_call_target="tpu_custom_call" | custom-call | flops 2147483648 | bytes 10000000 | tf_op jit(solution)/shard_map/mix/pallas_call | solution.py:317
  (4 shorter events, 0.0 us)
Async XLA Ops:
  7.2 126.5 %all-gather.3.cloned.1.call-start = ((), (), s32[]{:S(2)}) async-start(), calls=%async_computation.1 | async-start | bytes 4718592 | tf_op jit(solution)/shard_map/all_gather | solution.py:380
  15.6 2.1 %copy-start = (bf16[32,528,128]{2,1,0:T(8,128)(2,1)}, bf16[32,528,128]{2,1,0:T(8,128)(2,1)S(1)}, u32[]{:S(2)}) copy-start(bf16[32,528,128]{2,1,0:T(8,128)(2,1)S(1)} %pick.1) | copy-start | bytes 12976132
  17.6 11.1 %copy-start.4 = (bf16[2048]{0:T(1024)(128)(2,1)S(1)}, bf16[2048]{0:T(1024)(128)(2,1)}, u32[]{:S(2)}) copy-start(bf16[2048]{0:T(1024)(128)(2,1)} %param.9) | copy-start | bytes 12292
  17.6 11.1 %copy-start.3 = (s32[4,2]{0,1:T(2,128)S(1)}, s32[4,2]{0,1:T(2,128)}, u32[]{:S(2)}) copy-start(s32[4,2]{0,1:T(2,128)} %param.14) | copy-start | bytes 100
  17.6 105.8 %all-to-all-start = ((bf16[32,528,128]{2,1,0:T(8,128)(2,1)}), bf16[32,528,128]{2,1,0:T(8,128)(2,1)}, u32[]{:S(2)}, u32[]{:S(2)}) async-start(bf16[32,528,128]{2,1,0:T(8,128)(2,1)} %copy-done), calls=%async_computation | async-start | bytes 8650752 | tf_op jit(solution)/shard_map/all_to_all | solution.py:368
  22.4 45.8 %collective-permute-start.3 = (bf16[256,1024]{1,0:T(8,128)(2,1)}, bf16[256,1024]{1,0:T(8,128)(2,1)S(1)}, u32[]{:S(2)}, u32[]{:S(2)}) collective-permute-start(bf16[256,1024]{1,0:T(8,128)(2,1)} %get-tuple-element.31), channel_id=1, source_target_pairs={{0,1},{1,2},{2,3},{3,0},{4,5},{5,6},{6,7},{7,4},{8,9},{9,10},{10,1... | collective-permute-start | bytes 1572872 | tf_op jit(solution)/shard_map/ppermute | solution.py:387
  24.8 63.1 %collective-permute-start.4 = (bf16[256,1024]{1,0:T(8,128)(2,1)}, bf16[256,1024]{1,0:T(8,128)(2,1)}, u32[]{:S(2)}, u32[]{:S(2)}) collective-permute-start(bf16[256,1024]{1,0:T(8,128)(2,1)} %get-tuple-element.31), channel_id=1, source_target_pairs={{0,2},{1,3},{2,0},{3,1},{4,6},{5,7},{6,4},{7,5},{8,10},{9,11},{10,... | collective-permute-start | bytes 1572872 | tf_op jit(solution)/shard_map/ppermute | solution.py:387
  27.3 60.5 %collective-permute-start.5 = (bf16[256,1024]{1,0:T(8,128)(2,1)}, bf16[256,1024]{1,0:T(8,128)(2,1)}, u32[]{:S(2)}, u32[]{:S(2)}) collective-permute-start(bf16[256,1024]{1,0:T(8,128)(2,1)} %get-tuple-element.31), channel_id=1, source_target_pairs={{0,3},{1,0},{2,1},{3,2},{4,7},{5,4},{6,5},{7,6},{8,11},{9,8},{10,9... | collective-permute-start | bytes 1572872 | tf_op jit(solution)/shard_map/ppermute | solution.py:387
  28.9 1.6 %copy-start.1 = (bf16[2048,512]{1,0:T(8,128)(2,1)S(1)}, bf16[2048,512]{1,0:T(8,128)(2,1)}, u32[]{:S(2)}) copy-start(bf16[2048,512]{1,0:T(8,128)(2,1)} %wq_ref.1) | copy-start | bytes 6291460
  30.5 1.0 copy-start.2
  41.3 66.1 %collective-permute-start = (bf16[256,512]{1,0:T(8,128)(2,1)S(1)}, bf16[256,512]{1,0:T(8,128)(2,1)S(1)}, u32[]{:S(2)}, u32[]{:S(2)}) collective-permute-start(bf16[256,512]{1,0:T(8,128)(2,1)S(1)} %attend.4), channel_id=1, source_target_pairs={{0,1},{1,2},{2,3},{3,0},{4,5},{5,6},{6,7},{7,4},{8,9},{9,10},{10,1... | collective-permute-start | bytes 786440 | tf_op jit(solution)/shard_map/ppermute | solution.py:403
  87.8 45.8 %collective-permute-start.6 = (bf16[256,1024]{1,0:T(8,128)(2,1)S(1)}, bf16[256,1024]{1,0:T(8,128)(2,1)}, u32[]{:S(2)}, u32[]{:S(2)}) collective-permute-start(bf16[256,1024]{1,0:T(8,128)(2,1)S(1)} %collective-permute-done.3.refs_7_), channel_id=1, source_target_pairs={{0,4},{4,0},{1,5},{5,1},{2,6},{6,2},{3,7},{7,3},{8,12},{12,8},{9,1... | collective-permute-start | bytes 1572872 | tf_op jit(solution)/shard_map/ppermute | solution.py:400
  87.8 45.8 %collective-permute-start.7 = (bf16[256,1024]{1,0:T(8,128)(2,1)}, bf16[256,1024]{1,0:T(8,128)(2,1)}, u32[]{:S(2)}, u32[]{:S(2)}) collective-permute-start(bf16[256,1024]{1,0:T(8,128)(2,1)} %collective-permute-done.4.refs_9_), channel_id=1, source_target_pairs={{0,4},{4,0},{1,5},{5,1},{2,6},{6,2},{3,7},{7,3},{8,12},{12,8},{9,1... | collective-permute-start | bytes 1572872 | tf_op jit(solution)/shard_map/ppermute | solution.py:400
  88.3 45.3 %collective-permute-start.8 = (bf16[256,1024]{1,0:T(8,128)(2,1)}, bf16[256,1024]{1,0:T(8,128)(2,1)}, u32[]{:S(2)}, u32[]{:S(2)}) collective-permute-start(bf16[256,1024]{1,0:T(8,128)(2,1)} %collective-permute-done.5.refs_11_), channel_id=1, source_target_pairs={{0,4},{4,0},{1,5},{5,1},{2,6},{6,2},{3,7},{7,3},{8,12},{12,8},{9,1... | collective-permute-start | bytes 1572872 | tf_op jit(solution)/shard_map/ppermute | solution.py:400
  88.3 45.3 %collective-permute-start.1 = (bf16[256,512]{1,0:T(8,128)(2,1)}, bf16[256,512]{1,0:T(8,128)(2,1)}, u32[]{:S(2)}, u32[]{:S(2)}) collective-permute-start(bf16[256,512]{1,0:T(8,128)(2,1)} %attend.5), channel_id=1, source_target_pairs={{0,2},{1,3},{2,0},{3,1},{4,6},{5,7},{6,4},{7,5},{8,10},{9,11},{10,... | collective-permute-start | bytes 786440 | tf_op jit(solution)/shard_map/ppermute | solution.py:403
  107.5 26.1 %collective-permute-start.2 = (bf16[256,512]{1,0:T(8,128)(2,1)}, bf16[256,512]{1,0:T(8,128)(2,1)}, u32[]{:S(2)}, u32[]{:S(2)}) collective-permute-start(bf16[256,512]{1,0:T(8,128)(2,1)} %attend.6), channel_id=1, source_target_pairs={{0,3},{1,0},{2,1},{3,2},{4,7},{5,4},{6,5},{7,6},{8,11},{9,8},{10,9... | collective-permute-start | bytes 786440 | tf_op jit(solution)/shard_map/ppermute | solution.py:403
Sparse Core Ops, SparseCore 0:
  10.2 90.7 all-gather.2
